TPU v7x, 256 devices: a whole 4x4x8 slice. The times are simulated.
256 devices in a mesh: lat: 16 (over x_lo, z), lon: 16 (over y, x_hi, core).
Axes of the slice: x: 4 (x_hi: 2, x_lo: 2; x = x_hi * 2 + x_lo), y: 4, z: 8, core: 2. Of those that a mesh axis runs over, the one named last changes fastest.
Arguments:
- field_in: bfloat16 [160, 1536, 512], P('lat', 'lon'), may hold values from -6 to 6
- kernel_taps: bfloat16 [3, 160, 3, 33], P(None, 'lat'), may hold values from -0.8984375 to 0.8984375
- row_reach: int32 [160], P('lat'), may hold values from 1 to 16, as said below
- mix_weight: bfloat16 [3, 512, 512], replicated, may hold values from -0.15625 to 0.15625
- up_weight: bfloat16 [512, 1024], replicated, may hold values from -0.25 to 0.25
- down_weight: bfloat16 [1024, 512], replicated, may hold values from -0.1875 to 0.1875
- cotangent: bfloat16 [160, 1536, 512], P('lat', 'lon'), may hold values from -6 to 6
Outputs:
- block_out: bfloat16 [160, 1536, 512], P('lat', 'lon')
- grad_field: bfloat16 [160, 1536, 512], P('lat', 'lon')
- grad_mix: bfloat16 [3, 512, 512], replicated
- grad_up: bfloat16 [512, 1024], replicated
- grad_down: bfloat16 [1024, 512], replicated
Inputs may be any that keep to these rules, and one draw needn't show every extreme that they name: `row_reach`: how many longitude cells each latitude row's kernel reaches on either side.
All inputs are finite; a program needn't handle non-finite values.
Results may differ from a plain program's by a relative error of at most 0.0068.
Values may be sent and summed in bfloat16 or wider, within the bound.
A program may use at most 128 MiB of HBM per device.

v0:
```python
import math

import jax
import jax.numpy as jnp
from jax import lax
from jax.sharding import PartitionSpec as P

inv_root_two = 0.7071067811865476
inv_root_tau = 0.3989422804014327


def extended_2(x, sides, width, wrap):
    for axis, dim in sides:
        devices, length = (lax.axis_size(axis), x.shape[dim])
        up = [(i, (i + 1) % devices) for i in range(devices if wrap else devices - 1)]
        down = [(j, i) for i, j in up]
        last = lax.slice_in_dim(x, length - width, length, axis=dim)
        leading = lax.slice_in_dim(x, 0, width, axis=dim)
        before = lax.ppermute(last, axis, up)
        after = lax.ppermute(leading, axis, down)
        x = jnp.concatenate([before, x, after], axis=dim)
    return x


def shifted(block, axis, distance):
    devices = range(lax.axis_size(axis))
    route = [((i - distance) % len(devices), i) for i in devices]
    return lax.ppermute(block, axis, route)


def gelu_exact(value):
    return 0.5 * value * (1.0 + jax.scipy.special.erf(value * inv_root_two))


def gelu_slope(value):
    return (
        0.5 * (1.0 + jax.scipy.special.erf(value * inv_root_two))
        + value * jnp.exp(-0.5 * value * value) * inv_root_tau
    )


def local(field_in, kernel_taps, row_reach, mix_weight, up_weight, down_weight, cotangent):
    lat_rows, lon_cols, channels = field_in.shape
    basis_count = kernel_taps.shape[0]
    tap_count = kernel_taps.shape[3]
    reach_cells = (tap_count - 1) // 2
    lat_count = lax.axis_size("lat")
    lon_count = lax.axis_size("lon")
    lat_place = lax.axis_index("lat")
    north_pole = lat_place == 0
    south_pole = lat_place == lat_count - 1
    first_pass = extended_2(field_in, (("lat", 0),), 1, False)
    extended = extended_2(first_pass, (("lon", 1),), reach_cells, True)
    across = shifted(jnp.stack([extended[1], extended[lat_rows]]), "lon", lon_count // 2)
    extended = extended.at[0].set(jnp.where(north_pole, across[0], extended[0]))
    extended = extended.at[lat_rows + 1].set(
        jnp.where(south_pole, across[1], extended[lat_rows + 1])
    )
    padded_width = lon_cols + 2 * reach_cells
    offsets = jnp.arange(tap_count, dtype=jnp.int32) - reach_cells
    tap_mask = jnp.abs(offsets)[None, :] <= row_reach[:, None]
    masked_taps = jnp.where(
        tap_mask[None, :, None, :], kernel_taps, jnp.zeros((), kernel_taps.dtype)
    )
    selector = (
        jnp.arange(padded_width, dtype=jnp.int32)[None, :, None]
        - jnp.arange(lon_cols, dtype=jnp.int32)[:, None, None]
        == jnp.arange(tap_count, dtype=jnp.int32)[None, None, :]
    ).astype(jnp.bfloat16)
    band_matrix = jnp.einsum(
        "krdt,jat->krjda", masked_taps, selector, preferred_element_type=jnp.float32
    ).astype(jnp.bfloat16)
    windows = jnp.stack(
        [extended[0:lat_rows], extended[1 : lat_rows + 1], extended[2 : lat_rows + 2]], axis=1
    )
    features = jnp.einsum(
        "krjda,rdac->krjc", band_matrix, windows, preferred_element_type=jnp.float32
    ).astype(jnp.bfloat16)
    points = lat_rows * lon_cols
    flat_features = features.reshape(basis_count, points, channels)
    flat_field = field_in.reshape(points, channels)
    conv_sum = jnp.einsum(
        "kpc,kcd->pd", flat_features, mix_weight, preferred_element_type=jnp.float32
    )
    hidden = (flat_field.astype(jnp.float32) + conv_sum).astype(jnp.bfloat16)
    pre_act = jnp.dot(hidden, up_weight, preferred_element_type=jnp.float32)
    activated = gelu_exact(pre_act).astype(jnp.bfloat16)
    block_out = (
        hidden.astype(jnp.float32)
        + jnp.dot(activated, down_weight, preferred_element_type=jnp.float32)
    ).astype(jnp.bfloat16)
    grad_rows = cotangent.reshape(points, channels)
    act_grad = lax.dot_general(
        grad_rows, down_weight, (((1,), (1,)), ((), ())), preferred_element_type=jnp.float32
    )
    pre_grad = (act_grad * gelu_slope(pre_act)).astype(jnp.bfloat16)
    down_local = lax.dot_general(
        activated, grad_rows, (((0,), (0,)), ((), ())), preferred_element_type=jnp.float32
    )
    up_local = lax.dot_general(
        hidden, pre_grad, (((0,), (0,)), ((), ())), preferred_element_type=jnp.float32
    )
    hidden_grad = (
        grad_rows.astype(jnp.float32)
        + lax.dot_general(
            pre_grad, up_weight, (((1,), (1,)), ((), ())), preferred_element_type=jnp.float32
        )
    ).astype(jnp.bfloat16)
    mix_local = jnp.einsum(
        "kpc,pd->kcd", flat_features, hidden_grad, preferred_element_type=jnp.float32
    )
    feat_grad = jnp.einsum(
        "pd,kcd->kpc", hidden_grad, mix_weight, preferred_element_type=jnp.float32
    ).astype(jnp.bfloat16)
    feat_grad_rows = feat_grad.reshape(basis_count, lat_rows, lon_cols, channels)
    spread = jnp.einsum(
        "krjda,krjc->rdac", band_matrix, feat_grad_rows, preferred_element_type=jnp.float32
    )
    pulled = (
        jnp.pad(spread[:, 0], ((0, 2), (0, 0), (0, 0)))
        + jnp.pad(spread[:, 1], ((1, 1), (0, 0), (0, 0)))
        + jnp.pad(spread[:, 2], ((2, 0), (0, 0), (0, 0)))
    )
    returned = shifted(
        jnp.stack([pulled[0], pulled[lat_rows + 1]]).astype(jnp.bfloat16), "lon", lon_count // 2
    ).astype(jnp.float32)
    pulled = pulled.at[1].add(jnp.where(north_pole, returned[0], jnp.zeros_like(returned[0])))
    pulled = pulled.at[lat_rows].add(
        jnp.where(south_pole, returned[1], jnp.zeros_like(returned[1]))
    )
    col_rims = jnp.concatenate(
        [pulled[:, :reach_cells], pulled[:, lon_cols + reach_cells :]], axis=1
    )
    col_edges = extended_2(col_rims.astype(jnp.bfloat16), (("lon", 1),), reach_cells, True).astype(
        col_rims.dtype
    )
    interior = pulled[:, reach_cells : reach_cells + lon_cols]
    interior = interior.at[:, :reach_cells].add(col_edges[:, :reach_cells])
    interior = interior.at[:, lon_cols - reach_cells :].add(col_edges[:, 3 * reach_cells :])
    row_edges = extended_2(
        jnp.stack([interior[0], interior[lat_rows + 1]]).astype(jnp.bfloat16),
        (("lat", 0),),
        1,
        False,
    ).astype(jnp.float32)
    adjoint = interior[1 : lat_rows + 1]
    adjoint = adjoint.at[0].add(row_edges[0])
    adjoint = adjoint.at[lat_rows - 1].add(row_edges[3])
    grad_field = (
        hidden_grad.astype(jnp.float32).reshape(lat_rows, lon_cols, channels) + adjoint
    ).astype(jnp.bfloat16)
    grad_scale = 1.0 / math.sqrt(points * lat_count * lon_count)
    mix_total, up_total, down_total = lax.psum((mix_local, up_local, down_local), ("lat", "lon"))
    mix_out = (mix_total * grad_scale).astype(jnp.bfloat16)
    up_out = (up_total * grad_scale).astype(jnp.bfloat16)
    down_out = (down_total * grad_scale).astype(jnp.bfloat16)
    return (block_out.reshape(lat_rows, lon_cols, channels), grad_field, mix_out, up_out, down_out)


def solution(mesh):
    placed = (
        P("lat", "lon", None),
        P(None, "lat", None, None),
        P("lat"),
        P(),
        P(),
        P(),
        P("lat", "lon", None),
    )
    return jax.shard_map(
        local,
        mesh=mesh,
        in_specs=placed,
        out_specs=(P("lat", "lon", None), P("lat", "lon", None), P(), P(), P()),
        check_vma=False,
    )
```

profile of v0, /device:TPU:1, one launch (start us, length us, event | category | flops | bytes accessed | tf_op | source)
XLA Modules:
  0.0 364.7 jit_solution(5280903188768959156)
XLA Ops:
  7.2 1.1 fusion.45
  8.3 1.3 collective-permute-start.1
  9.6 5.0 %collective-permute-start = (bf16[1,96,512]{2,1,0:T(8,128)(2,1)S(1)}, bf16[1,96,512]{2,1,0:T(8,128)(2,1)S(1)}, u32[]{:S(2)}, u32[]{:S(2)}) collective-permute-start(bf16[1,96,512]{2,1,0:T(8,128)(2,1)S(1)} %get-tuple-element.123), channel_id=1, source_target_pairs={{0,16},{16,32},{32,48},{48,64},{64,80},{80,96},{96,112},{112,128},... | collective-permute-start | bytes 294920 | tf_op jit(solution)/shard_map/ppermute | solution.py:19
  14.6 0.7 broadcast_compare_fusion
  15.4 0.9 collective-permute-done
  16.2 1.3 constant_dynamic-update-slice_fusion.1
  17.6 4.3 %collective-permute-start.2 = (bf16[12,16,512]{2,1,0:T(8,128)(2,1)S(1)}, bf16[12,16,512]{2,1,0:T(8,128)(2,1)S(1)}, u32[]{:S(2)}, u32[]{:S(2)}) collective-permute-start(bf16[12,16,512]{2,1,0:T(8,128)(2,1)S(1)} %get-tuple-element.120), channel_id=1, source_target_pairs={{0,1},{1,2},{2,3},{3,4},{4,5},{5,6},{6,7},{7,8},{8,9},{9,10},{10,1... | collective-permute-start | bytes 589832 | tf_op jit(solution)/shard_map/ppermute | solution.py:19
  22.0 4.6 %collective-permute-done.2 = bf16[12,16,512]{2,1,0:T(8,128)(2,1)S(1)} collective-permute-done((bf16[12,16,512]{2,1,0:T(8,128)(2,1)S(1)}, bf16[12,16,512]{2,1,0:T(8,128)(2,1)S(1)}, u32[]{:S(2)}, u32[]{:S(2)}) %collective-permute-start.2) | collective-permute-done | bytes 196640 | tf_op jit(solution)/shard_map/ppermute | solution.py:19
  26.5 4.2 %collective-permute-done.3 = bf16[12,16,512]{2,1,0:T(8,128)(2,1)S(1)} collective-permute-done((bf16[12,16,512]{2,1,0:T(8,128)(2,1)S(1)}, bf16[12,16,512]{2,1,0:T(8,128)(2,1)S(1)}, u32[]{:S(2)}, u32[]{:S(2)}) %collective-permute-start.3) | collective-permute-done | bytes 196640 | tf_op jit(solution)/shard_map/ppermute | solution.py:20
  30.7 0.2 pad_maximum_fusion
  31.0 2.4 collective-permute-start.4
  33.4 1.1 convert_bitcast_fusion
  34.5 5.0 %collective-permute-done.4 = bf16[2,128,512]{2,1,0:T(8,128)(2,1)S(1)} collective-permute-done((bf16[2,128,512]{2,1,0:T(8,128)(2,1)S(1)}, bf16[2,128,512]{2,1,0:T(8,128)(2,1)S(1)}, u32[]{:S(2)}, u32[]{:S(2)}) %collective-permute-start.4) | collective-permute-done | bytes 262176 | tf_op jit(solution)/shard_map/ppermute | solution.py:28
  39.6 0.4 slice_bitcast_fusion.5
  40.0 1.9 fusion.11
  42.0 0.2 copy.25
  42.2 1.0 copy-done.6
  43.2 1.7 fusion.19
  45.0 4.1 %multiply_convert_fusion = (bf16[960,1024]{1,0:T(8,128)(2,1)S(1)}, f32[960,1024]{1,0:T(8,128)S(1)}) fusion(bf16[960,512]{1,0:T(8,128)(2,1)S(1)} %fusion.19, bf16[512,1024]{1,0:T(8,128)(2,1)S(1)} %copy-done.12), kind=kOutput, calls=%fused_computation.14 | convolution fusion | flops 1011548160 | bytes 7929856 | tf_op jit(solution)/shard_map/dot_general | solution.py:86
  49.1 2.5 fusion.5
  51.6 1.3 add_convert_fusion
  52.9 2.6 fusion.46
  55.5 3.5 fusion.22
  59.0 3.3 convolution_convert_fusion
  62.3 2.7 fusion.47
  65.0 4.1 %convolution_bitcast_fusion = f32[10,3,128,512]{3,2,0,1:T(8,128)S(1)} fusion(bf16[3,10,96,512]{3,2,1,0:T(8,128)(2,1)} %bitcast.83, bf16[3,10,96,3,128]{4,1,3,0,2:T(8,128)(2,1)S(1)} %copy-done.3), kind=kOutput, calls=%fused_computation.19 | convolution fusion | flops 1132462080 | bytes 13025280 | tf_op jit(solution)/shard_map/krjda,krjc->rdac/dot_general | solution.py:116
  69.1 3.7 %slice_bitcast_fusion.2 = (f32[10,128,512]{2,1,0:T(8,128)S(1)}, f32[10,128,512]{2,1,0:T(8,128)}, f32[10,128,512]{2,1,0:T(8,128)}) fusion(f32[10,3,128,512]{3,2,0,1:T(8,128)S(1)} %convolution_bitcast_fusion), kind=kLoop, calls=%fused_computation.25 | loop fusion | bytes 15728640 | tf_op jit(solution)/shard_map/squeeze | solution.py:120
  72.8 3.7 %fusion.39 = (bf16[12,128,512]{2,1,0:T(8,128)(2,1)S(1)}, f32[12,128,512]{2,1,0:T(8,128)S(1)}) fusion(f32[10,128,512]{2,1,0:T(8,128)} %get-tuple-element.108, f32[10,128,512]{2,1,0:T(8,128)} %get-tuple-element.107, f32[10,128,512]{2,1,0:T(8,128)S(1)} %get-tuple-element.106), kind=kLoop, calls=%fused_computation.83 | loop fusion | flops 2359296 | bytes 12582912 | tf_op jit(solution)/shard_map/convert.13
  76.6 3.6 collective-permute-start.5
  80.2 5.5 %collective-permute-done.5 = bf16[2,128,512]{2,1,0:T(8,128)(2,1)S(1)} collective-permute-done((bf16[2,128,512]{2,1,0:T(8,128)(2,1)S(1)}, bf16[2,128,512]{2,1,0:T(8,128)(2,1)S(1)}, u32[]{:S(2)}, u32[]{:S(2)}) %collective-permute-start.5) | collective-permute-done | bytes 262176 | tf_op jit(solution)/shard_map/ppermute | solution.py:28
  86.0 0.2 convert.21
  86.2 4.7 %collective-permute-start.6 = (bf16[12,16,512]{2,1,0:T(8,128)(2,1)S(1)}, bf16[12,16,512]{2,1,0:T(8,128)(2,1)S(1)}, u32[]{:S(2)}, u32[]{:S(2)}) collective-permute-start(bf16[12,16,512]{2,1,0:T(8,128)(2,1)S(1)} %get-tuple-element.109), channel_id=1, source_target_pairs={{0,1},{1,2},{2,3},{3,4},{4,5},{5,6},{6,7},{7,8},{8,9},{9,10},{10,1... | collective-permute-start | bytes 589832 | tf_op jit(solution)/shard_map/ppermute | solution.py:19
  90.9 0.2 slice.334
  91.1 2.5 collective-permute-done.6
  93.6 4.4 %collective-permute-done.7 = bf16[12,16,512]{2,1,0:T(8,128)(2,1)S(1)} collective-permute-done((bf16[12,16,512]{2,1,0:T(8,128)(2,1)S(1)}, bf16[12,16,512]{2,1,0:T(8,128)(2,1)S(1)}, u32[]{:S(2)}, u32[]{:S(2)}) %collective-permute-start.7) | collective-permute-done | bytes 196640 | tf_op jit(solution)/shard_map/ppermute | solution.py:20
  98.1 0.1 fusion.26
  98.2 0.2 convert.22
  98.4 2.1 collective-permute-start.8
  100.5 1.3 collective-permute-start.9
  101.8 2.1 add_convert_fusion.1
  104.0 0.2 slice.339
  104.1 3.0 collective-permute-done.9
  107.2 1.3 fusion.18
  108.5 242.5 %all-reduce.6.cloned.1.call-done = (f32[3,512,512]{2,1,0:T(8,128)}, f32[512,1024]{1,0:T(8,128)}, f32[1024,512]{1,0:T(8,128)}) async-done(((f32[3,512,512]{2,1,0:T(8,128)}, f32[512,1024]{1,0:T(8,128)}, f32[1024,512]{1,0:T(8,128)}), (f32[3,512,512]{2,1,0:T(8,128)}, f32[512,1024]{1,0:T(8,128)}, f32[1024,512]{1,0:T(8,128)})) %all-reduce.6.cloned.1.call-update) | async-done | bytes 7340048 | tf_op jit(solution)/shard_map/psum | solution.py:153
  351.0 3.6 multiply_convert_fusion.1
  354.6 1.2 multiply_convert_fusion.3
  355.9 0.7 copy-done.4
  356.6 1.3 multiply_convert_fusion.2
  (60 shorter events, 0.8 us)
Async XLA Ops:
  7.2 35.0 %copy-start = (bf16[3,512,512]{2,1,0:T(8,128)(2,1)S(1)}, bf16[3,512,512]{2,1,0:T(8,128)(2,1)}, u32[]{:S(2)}) copy-start(bf16[3,512,512]{2,1,0:T(8,128)(2,1)} %param.26) | copy-start | bytes 4718596
  7.2 14.8 %copy-start.11 = (bf16[3,10,3,33]{3,2,1,0:T(4,128)(2,1)S(1)}, bf16[3,10,3,33]{3,2,1,0:T(4,128)(2,1)}, u32[]{:S(2)}) copy-start(bf16[3,10,3,33]{3,2,1,0:T(4,128)(2,1)} %param.24) | copy-start | bytes 17824
  7.2 343.8 %all-reduce.6.cloned.1.call-start = ((), (), s32[]{:S(2)}) async-start(), calls=%async_computation | async-start | bytes 14680064 | tf_op jit(solution)/shard_map/psum | solution.py:153
  8.3 9.2 %collective-permute-start.1 = (bf16[1,96,512]{2,1,0:T(8,128)(2,1)S(1)}, bf16[1,96,512]{2,1,0:T(8,128)(2,1)S(1)}, u32[]{:S(2)}, u32[]{:S(2)}) collective-permute-start(bf16[1,96,512]{2,1,0:T(8,128)(2,1)S(1)} %get-tuple-element.122), channel_id=1, source_target_pairs={{16,0},{32,16},{48,32},{64,48},{80,64},{96,80},{112,96},{128,112},... | collective-permute-start | bytes 294920 | tf_op jit(solution)/shard_map/ppermute | solution.py:20
  9.6 6.6 %collective-permute-start = (bf16[1,96,512]{2,1,0:T(8,128)(2,1)S(1)}, bf16[1,96,512]{2,1,0:T(8,128)(2,1)S(1)}, u32[]{:S(2)}, u32[]{:S(2)}) collective-permute-start(bf16[1,96,512]{2,1,0:T(8,128)(2,1)S(1)} %get-tuple-element.123), channel_id=1, source_target_pairs={{0,16},{16,32},{32,48},{48,64},{64,80},{80,96},{96,112},{112,128},... | collective-permute-start | bytes 294920 | tf_op jit(solution)/shard_map/ppermute | solution.py:19
  17.6 8.9 %collective-permute-start.2 = (bf16[12,16,512]{2,1,0:T(8,128)(2,1)S(1)}, bf16[12,16,512]{2,1,0:T(8,128)(2,1)S(1)}, u32[]{:S(2)}, u32[]{:S(2)}) collective-permute-start(bf16[12,16,512]{2,1,0:T(8,128)(2,1)S(1)} %get-tuple-element.120), channel_id=1, source_target_pairs={{0,1},{1,2},{2,3},{3,4},{4,5},{5,6},{6,7},{7,8},{8,9},{9,10},{10,1... | collective-permute-start | bytes 589832 | tf_op jit(solution)/shard_map/ppermute | solution.py:19
  21.9 8.8 %collective-permute-start.3 = (bf16[12,16,512]{2,1,0:T(8,128)(2,1)S(1)}, bf16[12,16,512]{2,1,0:T(8,128)(2,1)S(1)}, u32[]{:S(2)}, u32[]{:S(2)}) collective-permute-start(bf16[12,16,512]{2,1,0:T(8,128)(2,1)S(1)} %get-tuple-element.121), channel_id=1, source_target_pairs={{1,0},{2,1},{3,2},{4,3},{5,4},{6,5},{7,6},{8,7},{9,8},{10,9},{11,1... | collective-permute-start | bytes 589832 | tf_op jit(solution)/shard_map/ppermute | solution.py:20
  31.0 8.5 %collective-permute-start.4 = (bf16[2,128,512]{2,1,0:T(8,128)(2,1)S(1)}, bf16[2,128,512]{2,1,0:T(8,128)(2,1)S(1)}, u32[]{:S(2)}, u32[]{:S(2)}) collective-permute-start(bf16[2,128,512]{2,1,0:T(8,128)(2,1)S(1)} %pad_maximum_fusion.1), channel_id=1, source_target_pairs={{8,0},{9,1},{10,2},{11,3},{12,4},{13,5},{14,6},{15,7},{0,8},{1,9},... | collective-permute-start | bytes 786440 | tf_op jit(solution)/shard_map/ppermute | solution.py:28
  34.5 5.6 %copy-start.2 = (bf16[3,10,96,3,128]{4,1,3,0,2:T(8,128)(2,1)}, bf16[3,10,96,3,128]{4,1,3,0,2:T(8,128)(2,1)S(1)}, u32[]{:S(2)}) copy-start(bf16[3,10,96,3,128]{4,1,3,0,2:T(8,128)(2,1)S(1)} %convert_bitcast_fusion) | copy-start | bytes 6635524
  42.0 1.2 copy-start.6
  43.2 1.7 copy-start.12
  44.9 8.0 %copy-start.7 = (bf16[960,512]{1,0:T(8,128)(2,1)}, bf16[960,512]{1,0:T(8,128)(2,1)S(1)}, u32[]{:S(2)}) copy-start(bf16[960,512]{1,0:T(8,128)(2,1)S(1)} %fusion.19) | copy-start | bytes 2949124
  44.9 4.2 %copy-start.13 = (bf16[1024,512]{1,0:T(8,128)(2,1)S(1)}, bf16[1024,512]{1,0:T(8,128)(2,1)}, u32[]{:S(2)}) copy-start(bf16[1024,512]{1,0:T(8,128)(2,1)} %param.28) | copy-start | bytes 3145732
  45.0 4.2 %copy-start.15 = (bf16[10,96,512]{2,1,0:T(8,128)(2,1)S(1)}, bf16[10,96,512]{2,1,0:T(8,128)(2,1)}, u32[]{:S(2)}) copy-start(bf16[10,96,512]{2,1,0:T(8,128)(2,1)} %param.29) | copy-start | bytes 2949124
  49.1 13.2 %copy-start.16 = (bf16[960,1024]{1,0:T(8,128)(2,1)}, bf16[960,1024]{1,0:T(8,128)(2,1)S(1)}, u32[]{:S(2)}) copy-start(bf16[960,1024]{1,0:T(8,128)(2,1)S(1)} %get-tuple-element.124) | copy-start | bytes 5898244
  52.9 6.1 %copy-start.9 = (bf16[960,512]{1,0:T(8,128)(2,1)}, bf16[960,512]{1,0:T(8,128)(2,1)S(1)}, u32[]{:S(2)}) copy-start(bf16[960,512]{1,0:T(8,128)(2,1)S(1)} %add_convert_fusion) | copy-start | bytes 2949124
  62.3 2.7 copy-start.3
  76.6 9.2 %collective-permute-start.5 = (bf16[2,128,512]{2,1,0:T(8,128)(2,1)S(1)}, bf16[2,128,512]{2,1,0:T(8,128)(2,1)S(1)}, u32[]{:S(2)}, u32[]{:S(2)}) collective-permute-start(bf16[2,128,512]{2,1,0:T(8,128)(2,1)S(1)} %pad_maximum_fusion.2), channel_id=1, source_target_pairs={{8,0},{9,1},{10,2},{11,3},{12,4},{13,5},{14,6},{15,7},{0,8},{1,9},... | collective-permute-start | bytes 786440 | tf_op jit(solution)/shard_map/ppermute | solution.py:28
  86.2 7.4 %collective-permute-start.6 = (bf16[12,16,512]{2,1,0:T(8,128)(2,1)S(1)}, bf16[12,16,512]{2,1,0:T(8,128)(2,1)S(1)}, u32[]{:S(2)}, u32[]{:S(2)}) collective-permute-start(bf16[12,16,512]{2,1,0:T(8,128)(2,1)S(1)} %get-tuple-element.109), channel_id=1, source_target_pairs={{0,1},{1,2},{2,3},{3,4},{4,5},{5,6},{6,7},{7,8},{8,9},{9,10},{10,1... | collective-permute-start | bytes 589832 | tf_op jit(solution)/shard_map/ppermute | solution.py:19
  90.9 7.1 %collective-permute-start.7 = (bf16[12,16,512]{2,1,0:T(8,128)(2,1)S(1)}, bf16[12,16,512]{2,1,0:T(8,128)(2,1)S(1)}, u32[]{:S(2)}, u32[]{:S(2)}) collective-permute-start(bf16[12,16,512]{2,1,0:T(8,128)(2,1)S(1)} %get-tuple-element.110), channel_id=1, source_target_pairs={{1,0},{2,1},{3,2},{4,3},{5,4},{6,5},{7,6},{8,7},{9,8},{10,9},{11,1... | collective-permute-start | bytes 589832 | tf_op jit(solution)/shard_map/ppermute | solution.py:20
  98.0 3.8 %copy-start.17 = (bf16[960,1024]{1,0:T(8,128)(2,1)S(1)}, bf16[960,1024]{1,0:T(8,128)(2,1)}, u32[]{:S(2)}) copy-start(bf16[960,1024]{1,0:T(8,128)(2,1)} %copy-done.16) | copy-start | bytes 5898244
  98.2 3.7 %copy-start.8 = (bf16[960,512]{1,0:T(8,128)(2,1)S(1)}, bf16[960,512]{1,0:T(8,128)(2,1)}, u32[]{:S(2)}) copy-start(bf16[960,512]{1,0:T(8,128)(2,1)} %copy-done.7) | copy-start | bytes 2949124
  98.2 3.7 %copy-start.14 = (bf16[1024,512]{1,0:T(8,128)(2,1)S(1)}, bf16[1024,512]{1,0:T(8,128)(2,1)}, u32[]{:S(2)}) copy-start(bf16[1024,512]{1,0:T(8,128)(2,1)} %param.28) | copy-start | bytes 3145732
  98.4 5.8 %collective-permute-start.8 = (bf16[1,96,512]{2,1,0:T(8,128)(2,1)S(1)}, bf16[1,96,512]{2,1,0:T(8,128)(2,1)S(1)}, u32[]{:S(2)}, u32[]{:S(2)}) collective-permute-start(bf16[1,96,512]{2,1,0:T(8,128)(2,1)S(1)} %get-tuple-element.118), channel_id=1, source_target_pairs={{0,16},{16,32},{32,48},{48,64},{64,80},{80,96},{96,112},{112,128},... | collective-permute-start | bytes 294920 | tf_op jit(solution)/shard_map/ppermute | solution.py:19
  100.5 6.6 %collective-permute-start.9 = (bf16[1,96,512]{2,1,0:T(8,128)(2,1)S(1)}, bf16[1,96,512]{2,1,0:T(8,128)(2,1)S(1)}, u32[]{:S(2)}, u32[]{:S(2)}) collective-permute-start(bf16[1,96,512]{2,1,0:T(8,128)(2,1)S(1)} %get-tuple-element.119), channel_id=1, source_target_pairs={{16,0},{32,16},{48,32},{64,48},{80,64},{96,80},{112,96},{128,112},... | collective-permute-start | bytes 294920 | tf_op jit(solution)/shard_map/ppermute | solution.py:20
  104.0 3.2 copy-start.10
  351.0 3.6 copy-start.5
  354.6 2.0 copy-start.4
  354.6 3.2 copy-start.1
Sparse Core Ops, SparseCore 0:
  72.9 278.0 all-reduce.5
where the time goes:
time: 366 us; the launch traced here: 365 us
  waiting for transfers between devices  273 us (75%)
  matrix products  30.9 us (8%)
  starting transfers between devices  24.8 us (7%)
  between operations  14.5 us (4%)
  other arithmetic  13 us (4%)
  local copies, waits for them, and re-layouts  8.96 us (2%)
    psum x1, waiting for transfers between devices, local(): lax.psum((mix_local, up_local, down_local), ('lat', 'lon'))  243 us
    ppermute x4, starting transfers between devices, extended_2(): before = lax.ppermute(last, axis, up)  16.2 us
    ppermute x4, waiting for transfers between devices, extended_2(): after = lax.ppermute(leading, axis, down)  11.6 us
    ppermute x2, waiting for transfers between devices, shifted(): return lax.ppermute(block, axis, route)  10.5 us
    ppermute x4, waiting for transfers between devices, extended_2(): before = lax.ppermute(last, axis, up)  7.87 us
  transfers between devices with their start and end apart: 11, of which 9 were waited for; matrix products, arithmetic and copies ran while one was open for 3% of the time, Pallas kernels for 0%

commit v1 on v0

--- a/solution.py
+++ b/solution.py
@@ -3,10 +3,251 @@
 import jax
 import jax.numpy as jnp
 from jax import lax
+from jax.experimental import pallas as pl
+from jax.experimental.pallas import tpu as pltpu
 from jax.sharding import PartitionSpec as P
 
 inv_root_two = 0.7071067811865476
 inv_root_tau = 0.3989422804014327
+
+
+MESH = pl.DeviceIdType.MESH
+ring_xy = 4
+ring_z = 8
+lanes = 512
+
+
+def multiple(value, of):
+    return pl.multiple_of(value, of)
+
+
+def remote(src, dst, send_sem, recv_sem, device):
+    return pltpu.make_async_remote_copy(
+        src_ref=src, dst_ref=dst, send_sem=send_sem, recv_sem=recv_sem, device_id=device, device_id_type=MESH
+    )
+
+
+class Place:
+    def __init__(self):
+        self.lat = lax.axis_index("lat")
+        self.lon = lax.axis_index("lon")
+        self.z = lax.rem(self.lat, ring_z)
+        self.core = lax.rem(self.lon, 2)
+        self.y = lax.div(self.lon, 4)
+        self.x = lax.rem(lax.div(self.lon, 2), 2) * 2 + lax.div(self.lat, ring_z)
+        self.first = self.x * (1 - self.core) + self.y * self.core
+        self.second = self.y * (1 - self.core) + self.x * self.core
+
+    def device(self, x, y, z, core):
+        return (lax.rem(x, 2) * ring_z + z, y * 4 + lax.div(x, 2) * 2 + core)
+
+    def partner(self):
+        return self.device(self.x, self.y, self.z, 1 - self.core)
+
+    def along_x(self, step):
+        return self.device(lax.rem(self.x + step, ring_xy), self.y, self.z, self.core)
+
+    def along_y(self, step):
+        return self.device(self.x, lax.rem(self.y + step, ring_xy), self.z, self.core)
+
+    def along_z(self, step):
+        return self.device(self.x, self.y, lax.rem(self.z + step, ring_z), self.core)
+
+    def along_first(self, step):
+        x = lax.rem(self.x + step * (1 - self.core), ring_xy)
+        y = lax.rem(self.y + step * self.core, ring_xy)
+        return self.device(x, y, self.z, self.core)
+
+    def along_second(self, step):
+        x = lax.rem(self.x + step * self.core, ring_xy)
+        y = lax.rem(self.y + step * (1 - self.core), ring_xy)
+        return self.device(x, y, self.z, self.core)
+
+    def everyone(self):
+        found = [self.partner()]
+        found += [self.along_x(s) for s in range(1, ring_xy)]
+        found += [self.along_y(s) for s in range(1, ring_xy)]
+        found += [self.along_z(s) for s in range(1, ring_z)]
+        return found
+
+
+def add_rows(dst, dst_at, sources, count, chunk):
+    def body(i, carry):
+        total = None
+        for ref, at in sources:
+            term = ref[pl.ds(multiple(at + i * chunk, 16), chunk), :].astype(jnp.float32)
+            total = term if total is None else total + term
+        dst[pl.ds(multiple(dst_at + i * chunk, 16), chunk), :] = total.astype(dst.dtype)
+        return carry
+
+    lax.fori_loop(0, count // chunk, body, 0)
+
+
+wire_steps = (2, 1, 3)
+z_steps = (4, 3, 5, 2, 6, 1, 7)
+
+
+class Reduction:
+    def __init__(self, place, rows, grad, out, parts, send, recv, scale):
+        self.p = place
+        self.rows = rows
+        self.half, self.quarter, self.piece = rows // 2, rows // 8, rows // 32
+        self.grad, self.out, self.scale = grad, out, scale
+        self.r0, self.s0, self.r1, self.s1, self.r2, self.s2, self.r3, self.zbuf = parts
+        self.send, self.recv = send, recv
+        self.used = 0
+        self.sent = []
+
+    @staticmethod
+    def scratch(rows):
+        half, quarter, piece = rows // 2, rows // 8, rows // 32
+        shapes = [
+            (half, lanes), (half, lanes), (3, quarter, lanes), (quarter, lanes),
+            (3, piece, lanes), (64, lanes), (7, 16, 256), (64, lanes),
+        ]
+        return [pltpu.VMEM(s, jnp.bfloat16) for s in shapes]
+
+    def go(self, src, dst, device):
+        copy = remote(src, dst, self.send.at[self.used], self.recv.at[self.used], device)
+        self.used += 1
+        copy.start()
+        self.sent.append(copy)
+        return copy
+
+    def start_pair(self):
+        p = self.p
+        other = multiple((1 - p.core) * self.half, 16)
+        self.flight = [self.go(self.grad.at[pl.ds(other, self.half), :], self.r0, p.partner())]
+
+    def arrived(self):
+        for copy in self.flight:
+            copy.wait_recv()
+        self.flight = []
+
+    def pair_then_first(self):
+        p = self.p
+        self.arrived()
+        flight = []
+        for step in (2, 1, 3, 0):
+            at = lax.rem(p.first + step, ring_xy) * self.quarter
+            add_rows(self.s0, at, [(self.grad, p.core * self.half + at), (self.r0, at)], self.quarter, 32)
+            if step:
+                src = self.s0.at[pl.ds(multiple(at, 16), self.quarter), :]
+                flight.append(self.go(src, self.r1.at[step - 1], p.along_first(step)))
+        self.flight = flight
+
+    def first_then_second(self):
+        p = self.p
+        self.arrived()
+        flight = []
+        own = p.first * self.quarter
+        for step in (2, 1, 3, 0):
+            at = lax.rem(p.second + step, ring_xy) * self.piece
+            sources = [(self.s0, own + at)] + [(self.r1.at[i], at) for i in range(3)]
+            add_rows(self.s1, at, sources, self.piece, 16)
+            if step:
+                src = self.s1.at[pl.ds(multiple(at, 16), self.piece), :]
+                flight.append(self.go(src, self.r2.at[step - 1], p.along_second(step)))
+        self.flight = flight
+
+    def spot(self, ref, index):
+        row = multiple(lax.div(index, 2) * 16, 16)
+        lane = multiple(lax.rem(index, 2) * 256, 256)
+        return ref.at[pl.ds(row, 16), pl.ds(lane, 256)]
+
+    def second_then_z(self):
+        p = self.p
+        self.arrived()
+        sources = [(self.s1, p.second * self.piece)] + [(self.r2.at[i], 0) for i in range(3)]
+        add_rows(self.s2, 0, sources, self.piece, 16)
+        if self.piece < 64:
+            self.s2[self.piece :, :] = jnp.zeros((64 - self.piece, lanes), jnp.bfloat16)
+        flight = []
+        for step in z_steps:
+            src = self.spot(self.s2, lax.rem(p.z + step, ring_z))
+            flight.append(self.go(src, self.r3.at[step - 1], p.along_z(step)))
+        self.flight = flight
+
+    def z_then_back(self):
+        p = self.p
+        self.arrived()
+        total = self.spot(self.s2, p.z)[...].astype(jnp.float32)
+        for i in range(7):
+            total = total + self.r3[i].astype(jnp.float32)
+        mine = self.spot(self.zbuf, p.z)
+        mine[...] = (total * self.scale).astype(jnp.bfloat16)
+        self.flight = [self.go(mine, mine, p.along_z(step)) for step in z_steps]
+
+    def back_second(self):
+        p = self.p
+        self.arrived()
+        at = p.core * self.half + p.first * self.quarter + p.second * self.piece
+        mine = self.out.at[pl.ds(multiple(at, 16), self.piece), :]
+        mine[...] = self.zbuf[: self.piece, :]
+        self.flight = [self.go(mine, mine, p.along_second(step)) for step in wire_steps]
+
+    def back_first(self):
+        p = self.p
+        self.arrived()
+        at = p.core * self.half + p.first * self.quarter
+        mine = self.out.at[pl.ds(multiple(at, 16), self.quarter), :]
+        self.flight = [self.go(mine, mine, p.along_first(step)) for step in wire_steps]
+
+    def back_pair(self):
+        p = self.p
+        self.arrived()
+        mine = self.out.at[pl.ds(multiple(p.core * self.half, 16), self.half), :]
+        self.flight = [self.go(mine, mine, p.partner())]
+
+    def finish(self):
+        self.arrived()
+        for copy in self.sent:
+            copy.wait_send()
+
+
+copies_each = 28
+
+
+def meet(devices):
+    barrier = pltpu.get_barrier_semaphore()
+    for device in devices:
+        pl.semaphore_signal(barrier, inc=1, device_id=device, device_id_type=MESH)
+    pl.semaphore_wait(barrier, len(devices))
+
+
+def sum_kernel(scale, mlp_ref, mix_ref, mlp_out, mix_out, *rest):
+    place = Place()
+    parts, sems = rest[:16], rest[16:]
+    meet(place.everyone())
+    mlp = Reduction(place, mlp_ref.shape[0], mlp_ref, mlp_out, parts[:8], sems[0], sems[1], scale)
+    mix = Reduction(place, mix_ref.shape[0], mix_ref, mix_out, parts[8:], sems[2], sems[3], scale)
+    both = (mlp, mix)
+    for stage in (
+        "start_pair", "pair_then_first", "first_then_second", "second_then_z", "z_then_back",
+        "back_second", "back_first", "back_pair", "finish",
+    ):
+        for item in both:
+            getattr(item, stage)()
+
+
+def sum_everywhere(mlp, mix, scale):
+    whole = pl.BlockSpec(memory_space=pltpu.VMEM)
+    return pl.pallas_call(
+        lambda *refs: sum_kernel(scale, *refs),
+        out_shape=(
+            jax.ShapeDtypeStruct(mlp.shape, jnp.bfloat16),
+            jax.ShapeDtypeStruct(mix.shape, jnp.bfloat16),
+        ),
+        in_specs=[whole, whole],
+        out_specs=(whole, whole),
+        scratch_shapes=Reduction.scratch(mlp.shape[0])
+        + Reduction.scratch(mix.shape[0])
+        + [pltpu.SemaphoreType.DMA((copies_each,)) for _ in range(4)],
+        compiler_params=pltpu.CompilerParams(
+            collective_id=0, has_side_effects=True, vmem_limit_bytes=60 * 1024 * 1024
+        ),
+        name="weight_sums",
+    )(mlp, mix)
 
 
 def extended_2(x, sides, width, wrap):
@@ -150,10 +391,14 @@
         hidden_grad.astype(jnp.float32).reshape(lat_rows, lon_cols, channels) + adjoint
     ).astype(jnp.bfloat16)
     grad_scale = 1.0 / math.sqrt(points * lat_count * lon_count)
-    mix_total, up_total, down_total = lax.psum((mix_local, up_local, down_local), ("lat", "lon"))
-    mix_out = (mix_total * grad_scale).astype(jnp.bfloat16)
-    up_out = (up_total * grad_scale).astype(jnp.bfloat16)
-    down_out = (down_total * grad_scale).astype(jnp.bfloat16)
+    mlp_rows = jnp.concatenate(
+        [up_local[:, :channels], up_local[:, channels:], down_local], axis=0
+    ).astype(jnp.bfloat16)
+    mix_rows = mix_local.astype(jnp.bfloat16).reshape(basis_count * channels, channels)
+    mlp_out, mix_out = sum_everywhere(mlp_rows, mix_rows, grad_scale)
+    up_out = jnp.concatenate([mlp_out[:channels], mlp_out[channels : 2 * channels]], axis=1)
+    down_out = mlp_out[2 * channels :]
+    mix_out = mix_out.reshape(basis_count, channels, channels)
     return (block_out.reshape(lat_rows, lon_cols, channels), grad_field, mix_out, up_out, down_out)
 
 

time: 366 us -> 158 us (0.43)
  waiting for transfers between devices: 273 us -> 30.2 us
  Pallas kernels: 0 us -> 60.7 us
  between operations: 14.5 us -> 1.18 us
  other arithmetic: 13 us -> 6.91 us
  starting transfers between devices: 24.8 us -> 20.7 us
    psum x1 -> x0, waiting for transfers between devices: 243 us -> none  [local(): lax.psum((mix_local, up_local, down_local), ('lat', 'lon'))]
    pallas_call x0 -> x1, Pallas kernels: none -> 60.7 us  [sum_everywhere(): pl.pallas_call(lambda *refs: sum_kernel(scale, *refs), out_shape=(jax.Sha...]
    convert_element_type x3 -> x0, other arithmetic: 6.12 us -> none  [the longest x1 3.61 us: local(): mix_out = (mix_total * grad_scale).astype(jnp.bfloat16)]
  transfers between devices with their start and end apart: 11 -> 10, of which waited for: 9 -> 8; matrix products, arithmetic and copies ran while one was open for 3% -> 4% of each run, Pallas kernels for 0% -> 0%
where the time goes in v1:
time: 158 us; the launch traced here: 157 us
  Pallas kernels  60.7 us (38%)
  waiting for transfers between devices  30.2 us (19%)
  matrix products  27.5 us (17%)
  starting transfers between devices  20.7 us (13%)
  local copies, waits for them, and re-layouts  9.6 us (6%)
  other arithmetic  6.91 us (4%)
    pallas_call x1, Pallas kernels, sum_everywhere(): pl.pallas_call(lambda *refs: sum_kernel(scale, *refs), out_shape=(jax.Sha...  60.7 us
    ppermute x4, starting transfers between devices, extended_2(): before = lax.ppermute(last, axis, up)  14.1 us
    ppermute x4, waiting for transfers between devices, extended_2(): after = lax.ppermute(leading, axis, down)  11.5 us
    ppermute x2, waiting for transfers between devices, shifted(): return lax.ppermute(block, axis, route)  11 us
    ppermute x4, waiting for transfers between devices, extended_2(): before = lax.ppermute(last, axis, up)  7.74 us
    dot_general x1, matrix products, local(): pre_act = jnp.dot(hidden, up_weight, preferred_element_type=jnp.float32)  4.12 us
    dot_general x1, matrix products, local(): jnp.einsum('krjda,krjc->rdac', band_matrix, feat_grad_rows, preferred_ele...  4.1 us
    ppermute x2, starting transfers between devices, shifted(): return lax.ppermute(block, axis, route)  3.99 us
  transfers between devices with their start and end apart: 10, of which 8 were waited for; matrix products, arithmetic and copies ran while one was open for 4% of the time, Pallas kernels for 0%

profile of v1, /device:TPU:1, one launch (start us, length us, event | category | flops | bytes accessed | tf_op | source)
XLA Modules:
  0.0 156.7 jit_solution(10222704314810297143)
XLA Ops:
  0.7 1.1 fusion.46
  1.7 1.3 collective-permute-start.1
  3.0 5.0 %collective-permute-start = (bf16[1,96,512]{2,1,0:T(8,128)(2,1)S(1)}, bf16[1,96,512]{2,1,0:T(8,128)(2,1)S(1)}, u32[]{:S(2)}, u32[]{:S(2)}) collective-permute-start(bf16[1,96,512]{2,1,0:T(8,128)(2,1)S(1)} %get-tuple-element.128), channel_id=1, source_target_pairs={{0,16},{16,32},{32,48},{48,64},{64,80},{80,96},{96,112},{112,128},... | collective-permute-start | bytes 294920 | tf_op jit(solution)/shard_map/ppermute | solution.py:260
  8.1 0.7 broadcast_compare_fusion
  8.8 0.9 collective-permute-done
  9.7 1.3 constant_dynamic-update-slice_fusion.1
  11.0 4.3 %collective-permute-start.2 = (bf16[12,16,512]{2,1,0:T(8,128)(2,1)S(1)}, bf16[12,16,512]{2,1,0:T(8,128)(2,1)S(1)}, u32[]{:S(2)}, u32[]{:S(2)}) collective-permute-start(bf16[12,16,512]{2,1,0:T(8,128)(2,1)S(1)} %get-tuple-element.123), channel_id=1, source_target_pairs={{0,1},{1,2},{2,3},{3,4},{4,5},{5,6},{6,7},{7,8},{8,9},{9,10},{10,1... | collective-permute-start | bytes 589832 | tf_op jit(solution)/shard_map/ppermute | solution.py:260
  15.4 4.6 %collective-permute-done.2 = bf16[12,16,512]{2,1,0:T(8,128)(2,1)S(1)} collective-permute-done((bf16[12,16,512]{2,1,0:T(8,128)(2,1)S(1)}, bf16[12,16,512]{2,1,0:T(8,128)(2,1)S(1)}, u32[]{:S(2)}, u32[]{:S(2)}) %collective-permute-start.2) | collective-permute-done | bytes 196640 | tf_op jit(solution)/shard_map/ppermute | solution.py:260
  20.0 4.2 %collective-permute-done.3 = bf16[12,16,512]{2,1,0:T(8,128)(2,1)S(1)} collective-permute-done((bf16[12,16,512]{2,1,0:T(8,128)(2,1)S(1)}, bf16[12,16,512]{2,1,0:T(8,128)(2,1)S(1)}, u32[]{:S(2)}, u32[]{:S(2)}) %collective-permute-start.3) | collective-permute-done | bytes 196640 | tf_op jit(solution)/shard_map/ppermute | solution.py:261
  24.2 0.2 pad_maximum_fusion.1
  24.4 2.6 %collective-permute-start.4 = (bf16[2,128,512]{2,1,0:T(8,128)(2,1)S(1)}, bf16[2,128,512]{2,1,0:T(8,128)(2,1)S(1)}, u32[]{:S(2)}, u32[]{:S(2)}) collective-permute-start(bf16[2,128,512]{2,1,0:T(8,128)(2,1)S(1)} %pad_maximum_fusion.3), channel_id=1, source_target_pairs={{8,0},{9,1},{10,2},{11,3},{12,4},{13,5},{14,6},{15,7},{0,8},{1,9},... | collective-permute-start | bytes 786440 | tf_op jit(solution)/shard_map/ppermute | solution.py:269
  27.0 1.1 convert_bitcast_fusion
  28.1 5.0 %collective-permute-done.4 = bf16[2,128,512]{2,1,0:T(8,128)(2,1)S(1)} collective-permute-done((bf16[2,128,512]{2,1,0:T(8,128)(2,1)S(1)}, bf16[2,128,512]{2,1,0:T(8,128)(2,1)S(1)}, u32[]{:S(2)}, u32[]{:S(2)}) %collective-permute-start.4) | collective-permute-done | bytes 262176 | tf_op jit(solution)/shard_map/ppermute | solution.py:269
  33.2 0.4 slice_bitcast_fusion.5
  33.7 1.9 %fusion.11 = bf16[3,10,96,512]{3,2,0,1:T(8,128)(2,1)S(1)} fusion(bf16[3,10,96,3,128]{4,1,3,0,2:T(8,128)(2,1)S(1)} %convert_bitcast_fusion, bf16[10,1,128,512]{3,2,1,0:T(8,128)(2,1)S(1)} %get-tuple-element.117, bf16[10,1,128,512]{3,2,1,0:T(8,128)(2,1)S(1)} %get-tuple-element.118, bf16[10,1,128,512]{3,2,1,0:T(8,128)(2,1)S(1)} %get-tuple-element.116), kind=kOutput, calls=%fused_computation.19 | convolution fusion | flops 1145733120 | bytes 9093120 | tf_op jit(solution)/shard_map/krjda,rdac->krjc/dot_general | solution.py:317
  35.6 0.2 copy.25
  35.8 1.0 copy-done.6
  36.8 1.7 %fusion.19 = bf16[960,512]{1,0:T(8,128)(2,1)S(1)} fusion(bf16[960,512]{1,0:T(8,128)(2,1)S(1)} %bitcast.88, bf16[3,960,512]{2,1,0:T(8,128)(2,1)S(1)} %bitcast.84, bf16[3,512,512]{2,1,0:T(8,128)(2,1)S(1)} %copy-done), kind=kOutput, calls=%fused_computation.32 | convolution fusion | flops 1511424000 | bytes 6488064 | tf_op jit(solution)/shard_map/kpc,kcd->pd/dot_general | solution.py:323
  38.6 4.1 %multiply_convert_fusion = (bf16[960,1024]{1,0:T(8,128)(2,1)S(1)}, f32[960,1024]{1,0:T(8,128)S(1)}) fusion(bf16[960,512]{1,0:T(8,128)(2,1)S(1)} %fusion.19, bf16[512,1024]{1,0:T(8,128)(2,1)S(1)} %copy-done.10), kind=kOutput, calls=%fused_computation.14 | convolution fusion | flops 1011548160 | bytes 7929856 | tf_op jit(solution)/shard_map/dot_general | solution.py:327
  42.7 2.3 %fusion.5 = bf16[960,1024]{1,0:T(8,128)(2,1)S(1)} fusion(f32[960,1024]{1,0:T(8,128)S(1)} %get-tuple-element.130, bf16[960,512]{1,0:T(8,128)(2,1)S(1)} %bitcast.90, bf16[1024,512]{1,0:T(8,128)(2,1)S(1)} %copy-done.11), kind=kOutput, calls=%fused_computation.7 | convolution fusion | flops 1016463360 | bytes 7929856 | tf_op jit(solution)/shard_map/dot_general | solution.py:334
  45.1 1.2 add_convert_fusion
  46.3 1.3 convolution_convert_fusion.3
  47.6 3.0 %convolution_convert_fusion.1 = bf16[3,512,512]{2,1,0:T(8,128)(2,1)} fusion(bf16[3,960,512]{2,1,0:T(8,128)(2,1)S(1)} %bitcast.85, bf16[960,512]{1,0:T(8,128)(2,1)S(1)} %add_convert_fusion), kind=kOutput, calls=%fused_computation.37 | convolution fusion | flops 1510735872 | bytes 5505024 | tf_op jit(solution)/shard_map/kpc,pd->kcd/dot_general | solution.py:350
  50.6 3.4 %convolution_convert_fusion = bf16[960,3,512]{2,0,1:T(8,128)(2,1)} fusion(bf16[3,512,512]{2,1,0:T(8,128)(2,1)S(1)} %copy-done, bf16[960,512]{1,0:T(8,128)(2,1)S(1)} %add_convert_fusion), kind=kOutput, calls=%fused_computation.27 | convolution fusion | flops 1511424000 | bytes 5505024 | tf_op jit(solution)/shard_map/pd,kcd->kpc/dot_general | solution.py:353
  53.9 1.3 convolution_convert_fusion.2
  55.3 1.4 pad_maximum_fusion.refs_0_
  56.8 60.7 %weight_sums.1 = (bf16[2048,512]{1,0:T(8,128)(2,1)}, bf16[1536,512]{1,0:T(8,128)(2,1)}) custom-call(bf16[2048,512]{1,0:T(8,128)(2,1)} %pad_maximum_fusion.refs_0_, bf16[1536,512]{1,0:T(8,128)(2,1)} %bitcast.86), custom_call_target="tpu_custom_call" | custom-call | tf_op jit(solution)/shard_map/weight_sums/pallas_call | solution.py:235
  117.5 2.3 %slice.335 = bf16[1024,512]{1,0:T(8,128)(2,1)} slice(bf16[2048,512]{1,0:T(8,128)(2,1)} %get-tuple-element.104), slice={[1024:2048], [0:512]} | slice | bytes 2097152 | tf_op jit(solution)/shard_map/slice | solution.py:400
  119.7 4.1 %convolution_bitcast_fusion = f32[10,3,128,512]{3,2,0,1:T(8,128)S(1)} fusion(bf16[3,10,96,512]{3,2,1,0:T(8,128)(2,1)} %bitcast.83, bf16[3,10,96,3,128]{4,1,3,0,2:T(8,128)(2,1)S(1)} %copy-done.3), kind=kOutput, calls=%fused_computation.18 | convolution fusion | flops 1132462080 | bytes 13025280 | tf_op jit(solution)/shard_map/krjda,krjc->rdac/dot_general | solution.py:357
  123.8 1.5 slice_bitcast_fusion.2
  125.3 1.2 fusion.38
  126.6 1.4 collective-permute-start.5
  128.0 2.1 %add_convert_fusion.1 = bf16[960,512]{1,0:T(8,128)(2,1)} fusion(bf16[960,512]{1,0:T(8,128)(2,1)S(1)} %copy-done.17, bf16[960,1024]{1,0:T(8,128)(2,1)S(1)} %copy-done.15, bf16[1024,512]{1,0:T(8,128)(2,1)S(1)} %copy-done.12), kind=kOutput, calls=%fused_computation.34 | convolution fusion | flops 1008107520 | bytes 4980736 | tf_op jit(solution)/shard_map/dot_general | solution.py:331
  130.2 5.9 %collective-permute-done.5 = bf16[2,128,512]{2,1,0:T(8,128)(2,1)S(1)} collective-permute-done((bf16[2,128,512]{2,1,0:T(8,128)(2,1)S(1)}, bf16[2,128,512]{2,1,0:T(8,128)(2,1)S(1)}, u32[]{:S(2)}, u32[]{:S(2)}) %collective-permute-start.5) | collective-permute-done | bytes 262176 | tf_op jit(solution)/shard_map/ppermute | solution.py:269
  136.3 0.2 convert.30
  136.6 2.1 %collective-permute-start.6 = (bf16[12,16,512]{2,1,0:T(8,128)(2,1)S(1)}, bf16[12,16,512]{2,1,0:T(8,128)(2,1)S(1)}, u32[]{:S(2)}, u32[]{:S(2)}) collective-permute-start(bf16[12,16,512]{2,1,0:T(8,128)(2,1)S(1)} %get-tuple-element.112), channel_id=1, source_target_pairs={{0,1},{1,2},{2,3},{3,4},{4,5},{5,6},{6,7},{7,8},{8,9},{9,10},{10,1... | collective-permute-start | bytes 589832 | tf_op jit(solution)/shard_map/ppermute | solution.py:260
  138.8 0.2 slice.356
  139.0 2.3 %collective-permute-done.6 = bf16[12,16,512]{2,1,0:T(8,128)(2,1)S(1)} collective-permute-done((bf16[12,16,512]{2,1,0:T(8,128)(2,1)S(1)}, bf16[12,16,512]{2,1,0:T(8,128)(2,1)S(1)}, u32[]{:S(2)}, u32[]{:S(2)}) %collective-permute-start.6) | collective-permute-done | bytes 196640 | tf_op jit(solution)/shard_map/ppermute | solution.py:260
  141.3 4.5 %collective-permute-done.7 = bf16[12,16,512]{2,1,0:T(8,128)(2,1)S(1)} collective-permute-done((bf16[12,16,512]{2,1,0:T(8,128)(2,1)S(1)}, bf16[12,16,512]{2,1,0:T(8,128)(2,1)S(1)}, u32[]{:S(2)}, u32[]{:S(2)}) %collective-permute-start.7) | collective-permute-done | bytes 196640 | tf_op jit(solution)/shard_map/ppermute | solution.py:261
  145.8 0.1 fusion.25
  145.9 0.2 convert.31
  146.1 2.6 %collective-permute-start.8 = (bf16[1,96,512]{2,1,0:T(8,128)(2,1)S(1)}, bf16[1,96,512]{2,1,0:T(8,128)(2,1)S(1)}, u32[]{:S(2)}, u32[]{:S(2)}) collective-permute-start(bf16[1,96,512]{2,1,0:T(8,128)(2,1)S(1)} %get-tuple-element.121), channel_id=1, source_target_pairs={{0,16},{16,32},{32,48},{48,64},{64,80},{80,96},{96,112},{112,128},... | collective-permute-start | bytes 294920 | tf_op jit(solution)/shard_map/ppermute | solution.py:260
  148.8 1.3 collective-permute-start.9
  150.1 1.1 pad_maximum_fusion.2
  151.2 0.2 slice.361
  151.3 2.8 %collective-permute-done.9 = bf16[1,96,512]{2,1,0:T(8,128)(2,1)S(1)} collective-permute-done((bf16[1,96,512]{2,1,0:T(8,128)(2,1)S(1)}, bf16[1,96,512]{2,1,0:T(8,128)(2,1)S(1)}, u32[]{:S(2)}, u32[]{:S(2)}) %collective-permute-start.9) | collective-permute-done | bytes 98336 | tf_op jit(solution)/shard_map/ppermute | solution.py:261
  154.2 1.3 fusion.18
  155.6 1.1 copy.65
  (61 shorter events, 0.9 us)
Async XLA Ops:
  0.6 35.2 %copy-start = (bf16[3,512,512]{2,1,0:T(8,128)(2,1)S(1)}, bf16[3,512,512]{2,1,0:T(8,128)(2,1)}, u32[]{:S(2)}) copy-start(bf16[3,512,512]{2,1,0:T(8,128)(2,1)} %param.26) | copy-start | bytes 4718596
  0.6 14.7 %copy-start.9 = (bf16[3,10,3,33]{3,2,1,0:T(4,128)(2,1)S(1)}, bf16[3,10,3,33]{3,2,1,0:T(4,128)(2,1)}, u32[]{:S(2)}) copy-start(bf16[3,10,3,33]{3,2,1,0:T(4,128)(2,1)} %param.24) | copy-start | bytes 17824
  1.7 9.2 %collective-permute-start.1 = (bf16[1,96,512]{2,1,0:T(8,128)(2,1)S(1)}, bf16[1,96,512]{2,1,0:T(8,128)(2,1)S(1)}, u32[]{:S(2)}, u32[]{:S(2)}) collective-permute-start(bf16[1,96,512]{2,1,0:T(8,128)(2,1)S(1)} %get-tuple-element.127), channel_id=1, source_target_pairs={{16,0},{32,16},{48,32},{64,48},{80,64},{96,80},{112,96},{128,112},... | collective-permute-start | bytes 294920 | tf_op jit(solution)/shard_map/ppermute | solution.py:261
  3.0 6.6 %collective-permute-start = (bf16[1,96,512]{2,1,0:T(8,128)(2,1)S(1)}, bf16[1,96,512]{2,1,0:T(8,128)(2,1)S(1)}, u32[]{:S(2)}, u32[]{:S(2)}) collective-permute-start(bf16[1,96,512]{2,1,0:T(8,128)(2,1)S(1)} %get-tuple-element.128), channel_id=1, source_target_pairs={{0,16},{16,32},{32,48},{48,64},{64,80},{80,96},{96,112},{112,128},... | collective-permute-start | bytes 294920 | tf_op jit(solution)/shard_map/ppermute | solution.py:260
  11.0 8.9 %collective-permute-start.2 = (bf16[12,16,512]{2,1,0:T(8,128)(2,1)S(1)}, bf16[12,16,512]{2,1,0:T(8,128)(2,1)S(1)}, u32[]{:S(2)}, u32[]{:S(2)}) collective-permute-start(bf16[12,16,512]{2,1,0:T(8,128)(2,1)S(1)} %get-tuple-element.123), channel_id=1, source_target_pairs={{0,1},{1,2},{2,3},{3,4},{4,5},{5,6},{6,7},{7,8},{8,9},{9,10},{10,1... | collective-permute-start | bytes 589832 | tf_op jit(solution)/shard_map/ppermute | solution.py:260
  15.4 8.8 %collective-permute-start.3 = (bf16[12,16,512]{2,1,0:T(8,128)(2,1)S(1)}, bf16[12,16,512]{2,1,0:T(8,128)(2,1)S(1)}, u32[]{:S(2)}, u32[]{:S(2)}) collective-permute-start(bf16[12,16,512]{2,1,0:T(8,128)(2,1)S(1)} %get-tuple-element.124), channel_id=1, source_target_pairs={{1,0},{2,1},{3,2},{4,3},{5,4},{6,5},{7,6},{8,7},{9,8},{10,9},{11,1... | collective-permute-start | bytes 589832 | tf_op jit(solution)/shard_map/ppermute | solution.py:261
  24.4 8.7 %collective-permute-start.4 = (bf16[2,128,512]{2,1,0:T(8,128)(2,1)S(1)}, bf16[2,128,512]{2,1,0:T(8,128)(2,1)S(1)}, u32[]{:S(2)}, u32[]{:S(2)}) collective-permute-start(bf16[2,128,512]{2,1,0:T(8,128)(2,1)S(1)} %pad_maximum_fusion.3), channel_id=1, source_target_pairs={{8,0},{9,1},{10,2},{11,3},{12,4},{13,5},{14,6},{15,7},{0,8},{1,9},... | collective-permute-start | bytes 786440 | tf_op jit(solution)/shard_map/ppermute | solution.py:269
  28.1 5.6 %copy-start.2 = (bf16[3,10,96,3,128]{4,1,3,0,2:T(8,128)(2,1)}, bf16[3,10,96,3,128]{4,1,3,0,2:T(8,128)(2,1)S(1)}, u32[]{:S(2)}) copy-start(bf16[3,10,96,3,128]{4,1,3,0,2:T(8,128)(2,1)S(1)} %convert_bitcast_fusion) | copy-start | bytes 6635524
  35.6 1.2 copy-start.6
  36.8 1.7 %copy-start.10 = (bf16[512,1024]{1,0:T(8,128)(2,1)S(1)}, bf16[512,1024]{1,0:T(8,128)(2,1)}, u32[]{:S(2)}) copy-start(bf16[512,1024]{1,0:T(8,128)(2,1)} %param.27) | copy-start | bytes 3145732
  38.5 7.8 %copy-start.16 = (bf16[960,512]{1,0:T(8,128)(2,1)}, bf16[960,512]{1,0:T(8,128)(2,1)S(1)}, u32[]{:S(2)}) copy-start(bf16[960,512]{1,0:T(8,128)(2,1)S(1)} %fusion.19) | copy-start | bytes 2949124
  38.6 4.2 %copy-start.11 = (bf16[1024,512]{1,0:T(8,128)(2,1)S(1)}, bf16[1024,512]{1,0:T(8,128)(2,1)}, u32[]{:S(2)}) copy-start(bf16[1024,512]{1,0:T(8,128)(2,1)} %param.28) | copy-start | bytes 3145732
  38.6 4.2 %copy-start.13 = (bf16[10,96,512]{2,1,0:T(8,128)(2,1)S(1)}, bf16[10,96,512]{2,1,0:T(8,128)(2,1)}, u32[]{:S(2)}) copy-start(bf16[10,96,512]{2,1,0:T(8,128)(2,1)} %param.29) | copy-start | bytes 2949124
  42.7 11.2 %copy-start.14 = (bf16[960,1024]{1,0:T(8,128)(2,1)}, bf16[960,1024]{1,0:T(8,128)(2,1)S(1)}, u32[]{:S(2)}) copy-start(bf16[960,1024]{1,0:T(8,128)(2,1)S(1)} %get-tuple-element.129) | copy-start | bytes 5898244
  46.3 4.3 %copy-start.7 = (bf16[960,512]{1,0:T(8,128)(2,1)}, bf16[960,512]{1,0:T(8,128)(2,1)S(1)}, u32[]{:S(2)}) copy-start(bf16[960,512]{1,0:T(8,128)(2,1)S(1)} %add_convert_fusion) | copy-start | bytes 2949124
  56.8 63.0 %copy-start.3 = (bf16[3,10,96,3,128]{4,1,3,0,2:T(8,128)(2,1)S(1)}, bf16[3,10,96,3,128]{4,1,3,0,2:T(8,128)(2,1)}, u32[]{:S(2)}) copy-start(bf16[3,10,96,3,128]{4,1,3,0,2:T(8,128)(2,1)} %copy-done.2) | copy-start | bytes 6635524
  125.3 2.7 %copy-start.12 = (bf16[1024,512]{1,0:T(8,128)(2,1)S(1)}, bf16[1024,512]{1,0:T(8,128)(2,1)}, u32[]{:S(2)}) copy-start(bf16[1024,512]{1,0:T(8,128)(2,1)} %param.28) | copy-start | bytes 3145732
  125.3 2.7 %copy-start.15 = (bf16[960,1024]{1,0:T(8,128)(2,1)S(1)}, bf16[960,1024]{1,0:T(8,128)(2,1)}, u32[]{:S(2)}) copy-start(bf16[960,1024]{1,0:T(8,128)(2,1)} %copy-done.14) | copy-start | bytes 5898244
  125.3 2.7 %copy-start.17 = (bf16[960,512]{1,0:T(8,128)(2,1)S(1)}, bf16[960,512]{1,0:T(8,128)(2,1)}, u32[]{:S(2)}) copy-start(bf16[960,512]{1,0:T(8,128)(2,1)} %copy-done.16) | copy-start | bytes 2949124
  126.6 9.5 %collective-permute-start.5 = (bf16[2,128,512]{2,1,0:T(8,128)(2,1)S(1)}, bf16[2,128,512]{2,1,0:T(8,128)(2,1)S(1)}, u32[]{:S(2)}, u32[]{:S(2)}) collective-permute-start(bf16[2,128,512]{2,1,0:T(8,128)(2,1)S(1)} %pad_maximum_fusion.4), channel_id=1, source_target_pairs={{8,0},{9,1},{10,2},{11,3},{12,4},{13,5},{14,6},{15,7},{0,8},{1,9},... | collective-permute-start | bytes 786440 | tf_op jit(solution)/shard_map/ppermute | solution.py:269
  136.3 2.4 %copy-start.4 = (bf16[2048,512]{1,0:T(8,128)(2,1)S(1)}, bf16[2048,512]{1,0:T(8,128)(2,1)}, u32[]{:S(2)}) copy-start(bf16[2048,512]{1,0:T(8,128)(2,1)} %get-tuple-element.104) | copy-start | bytes 6291460
  136.6 4.7 %collective-permute-start.6 = (bf16[12,16,512]{2,1,0:T(8,128)(2,1)S(1)}, bf16[12,16,512]{2,1,0:T(8,128)(2,1)S(1)}, u32[]{:S(2)}, u32[]{:S(2)}) collective-permute-start(bf16[12,16,512]{2,1,0:T(8,128)(2,1)S(1)} %get-tuple-element.112), channel_id=1, source_target_pairs={{0,1},{1,2},{2,3},{3,4},{4,5},{5,6},{6,7},{7,8},{8,9},{9,10},{10,1... | collective-permute-start | bytes 589832 | tf_op jit(solution)/shard_map/ppermute | solution.py:260
  138.7 7.1 %collective-permute-start.7 = (bf16[12,16,512]{2,1,0:T(8,128)(2,1)S(1)}, bf16[12,16,512]{2,1,0:T(8,128)(2,1)S(1)}, u32[]{:S(2)}, u32[]{:S(2)}) collective-permute-start(bf16[12,16,512]{2,1,0:T(8,128)(2,1)S(1)} %get-tuple-element.113), channel_id=1, source_target_pairs={{1,0},{2,1},{3,2},{4,3},{5,4},{6,5},{7,6},{8,7},{9,8},{10,9},{11,1... | collective-permute-start | bytes 589832 | tf_op jit(solution)/shard_map/ppermute | solution.py:261
  146.1 5.2 %collective-permute-start.8 = (bf16[1,96,512]{2,1,0:T(8,128)(2,1)S(1)}, bf16[1,96,512]{2,1,0:T(8,128)(2,1)S(1)}, u32[]{:S(2)}, u32[]{:S(2)}) collective-permute-start(bf16[1,96,512]{2,1,0:T(8,128)(2,1)S(1)} %get-tuple-element.121), channel_id=1, source_target_pairs={{0,16},{16,32},{32,48},{48,64},{64,80},{80,96},{96,112},{112,128},... | collective-permute-start | bytes 294920 | tf_op jit(solution)/shard_map/ppermute | solution.py:260
  148.8 5.4 %collective-permute-start.9 = (bf16[1,96,512]{2,1,0:T(8,128)(2,1)S(1)}, bf16[1,96,512]{2,1,0:T(8,128)(2,1)S(1)}, u32[]{:S(2)}, u32[]{:S(2)}) collective-permute-start(bf16[1,96,512]{2,1,0:T(8,128)(2,1)S(1)} %get-tuple-element.122), channel_id=1, source_target_pairs={{16,0},{32,16},{48,32},{64,48},{80,64},{96,80},{112,96},{128,112},... | collective-permute-start | bytes 294920 | tf_op jit(solution)/shard_map/ppermute | solution.py:261
  151.2 3.1 %copy-start.8 = (bf16[960,512]{1,0:T(8,128)(2,1)S(1)}, bf16[960,512]{1,0:T(8,128)(2,1)}, u32[]{:S(2)}) copy-start(bf16[960,512]{1,0:T(8,128)(2,1)} %copy-done.7) | copy-start | bytes 2949124
  154.1 1.4 copy-start.5
  154.2 2.5 %copy-start.1 = (bf16[3,512,512]{2,1,0:T(8,128)(2,1)S(1)}, bf16[3,512,512]{2,1,0:T(8,128)(2,1)}, u32[]{:S(2)}) copy-start(bf16[3,512,512]{2,1,0:T(8,128)(2,1)} %param.26) | copy-start | bytes 4718596

commit v2 on v1

v2 whole, which is shorter than its diff:
```python
import math

import jax
import jax.numpy as jnp
from jax import lax
from jax.experimental import pallas as pl
from jax.experimental.pallas import tpu as pltpu
from jax.sharding import PartitionSpec as P

inv_root_two = 0.7071067811865476
inv_root_tau = 0.3989422804014327

MESH = pl.DeviceIdType.MESH
ring_xy = 4
ring_z = 8
lanes = 512


def multiple(value, of):
    return pl.multiple_of(value, of)


def remote(src, dst, send_sem, recv_sem, device):
    return pltpu.make_async_remote_copy(
        src_ref=src, dst_ref=dst, send_sem=send_sem, recv_sem=recv_sem, device_id=device, device_id_type=MESH
    )


class Place:
    def __init__(self):
        self.lat = lax.axis_index("lat")
        self.lon = lax.axis_index("lon")
        self.z = lax.rem(self.lat, ring_z)
        self.core = lax.rem(self.lon, 2)
        self.y = lax.div(self.lon, 4)
        self.x = lax.rem(lax.div(self.lon, 2), 2) * 2 + lax.div(self.lat, ring_z)
        self.first = self.x * (1 - self.core) + self.y * self.core
        self.second = self.y * (1 - self.core) + self.x * self.core

    def device(self, x, y, z, core):
        return (lax.rem(x, 2) * ring_z + z, y * 4 + lax.div(x, 2) * 2 + core)

    def partner(self):
        return self.device(self.x, self.y, self.z, 1 - self.core)

    def along_x(self, step):
        return self.device(lax.rem(self.x + step, ring_xy), self.y, self.z, self.core)

    def along_y(self, step):
        return self.device(self.x, lax.rem(self.y + step, ring_xy), self.z, self.core)

    def along_z(self, step):
        return self.device(self.x, self.y, lax.rem(self.z + step, ring_z), self.core)

    def along_first(self, step):
        x = lax.rem(self.x + step * (1 - self.core), ring_xy)
        y = lax.rem(self.y + step * self.core, ring_xy)
        return self.device(x, y, self.z, self.core)

    def along_second(self, step):
        x = lax.rem(self.x + step * self.core, ring_xy)
        y = lax.rem(self.y + step * (1 - self.core), ring_xy)
        return self.device(x, y, self.z, self.core)

    def everyone(self):
        found = [self.partner()]
        found += [self.along_x(s) for s in range(1, ring_xy)]
        found += [self.along_y(s) for s in range(1, ring_xy)]
        found += [self.along_z(s) for s in range(1, ring_z)]
        return found


def add_rows(dst, dst_at, sources, count, chunk):
    def body(i, carry):
        total = None
        for ref, at in sources:
            term = ref[pl.ds(multiple(at + i * chunk, 16), chunk), :].astype(jnp.float32)
            total = term if total is None else total + term
        dst[pl.ds(multiple(dst_at + i * chunk, 16), chunk), :] = total.astype(dst.dtype)
        return carry

    lax.fori_loop(0, count // chunk, body, 0)


wire_steps = (2, 1, 3)
z_steps = (4, 3, 5, 2, 6, 1, 7)


class Reduction:
    def __init__(self, place, rows, grad, out, parts, send, recv, scale):
        self.p = place
        self.rows = rows
        self.half, self.quarter, self.piece = rows // 2, rows // 8, rows // 32
        self.grad, self.out, self.scale = grad, out, scale
        self.r0, self.s0, self.r1, self.s1, self.r2, self.s2, self.r3, self.zbuf = parts
        self.send, self.recv = send, recv
        self.used = 0
        self.sent = []

    @staticmethod
    def scratch(rows):
        half, quarter, piece = rows // 2, rows // 8, rows // 32
        shapes = [
            (half, lanes), (half, lanes), (3, quarter, lanes), (quarter, lanes),
            (3, piece, lanes), (64, lanes), (7, 16, 256), (64, lanes),
        ]
        return [pltpu.VMEM(s, jnp.bfloat16) for s in shapes]

    def go(self, src, dst, device):
        copy = remote(src, dst, self.send.at[self.used], self.recv.at[self.used], device)
        self.used += 1
        copy.start()
        self.sent.append(copy)
        return copy

    def start_pair(self):
        p = self.p
        other = multiple((1 - p.core) * self.half, 16)
        self.flight = [self.go(self.grad.at[pl.ds(other, self.half), :], self.r0, p.partner())]

    def arrived(self):
        for copy in self.flight:
            copy.wait_recv()
        self.flight = []

    def pair_then_first(self):
        p = self.p
        self.arrived()
        flight = []
        for step in (2, 1, 3, 0):
            at = lax.rem(p.first + step, ring_xy) * self.quarter
            add_rows(self.s0, at, [(self.grad, p.core * self.half + at), (self.r0, at)], self.quarter, 32)
            if step:
                src = self.s0.at[pl.ds(multiple(at, 16), self.quarter), :]
                flight.append(self.go(src, self.r1.at[step - 1], p.along_first(step)))
        self.flight = flight

    def first_then_second(self):
        p = self.p
        self.arrived()
        flight = []
        own = p.first * self.quarter
        for step in (2, 1, 3, 0):
            at = lax.rem(p.second + step, ring_xy) * self.piece
            sources = [(self.s0, own + at)] + [(self.r1.at[i], at) for i in range(3)]
            add_rows(self.s1, at, sources, self.piece, 16)
            if step:
                src = self.s1.at[pl.ds(multiple(at, 16), self.piece), :]
                flight.append(self.go(src, self.r2.at[step - 1], p.along_second(step)))
        self.flight = flight

    def spot(self, ref, index):
        row = multiple(lax.div(index, 2) * 16, 16)
        lane = multiple(lax.rem(index, 2) * 256, 256)
        return ref.at[pl.ds(row, 16), pl.ds(lane, 256)]

    def second_then_z(self):
        p = self.p
        self.arrived()
        sources = [(self.s1, p.second * self.piece)] + [(self.r2.at[i], 0) for i in range(3)]
        add_rows(self.s2, 0, sources, self.piece, 16)
        if self.piece < 64:
            self.s2[self.piece :, :] = jnp.zeros((64 - self.piece, lanes), jnp.bfloat16)
        flight = []
        for step in z_steps:
            src = self.spot(self.s2, lax.rem(p.z + step, ring_z))
            flight.append(self.go(src, self.r3.at[step - 1], p.along_z(step)))
        self.flight = flight

    def z_then_back(self):
        p = self.p
        self.arrived()
        total = self.spot(self.s2, p.z)[...].astype(jnp.float32)
        for i in range(7):
            total = total + self.r3[i].astype(jnp.float32)
        mine = self.spot(self.zbuf, p.z)
        mine[...] = (total * self.scale).astype(jnp.bfloat16)
        self.flight = [self.go(mine, mine, p.along_z(step)) for step in z_steps]

    def back_second(self):
        p = self.p
        self.arrived()
        at = p.core * self.half + p.first * self.quarter + p.second * self.piece
        mine = self.out.at[pl.ds(multiple(at, 16), self.piece), :]
        mine[...] = self.zbuf[: self.piece, :]
        self.flight = [self.go(mine, mine, p.along_second(step)) for step in wire_steps]

    def back_first(self):
        p = self.p
        self.arrived()
        at = p.core * self.half + p.first * self.quarter
        mine = self.out.at[pl.ds(multiple(at, 16), self.quarter), :]
        self.flight = [self.go(mine, mine, p.along_first(step)) for step in wire_steps]

    def back_pair(self):
        p = self.p
        self.arrived()
        mine = self.out.at[pl.ds(multiple(p.core * self.half, 16), self.half), :]
        self.flight = [self.go(mine, mine, p.partner())]

    def finish(self):
        self.arrived()
        for copy in self.sent:
            copy.wait_send()


copies_each = 28


rows = 10
cols = 96
reach = 16
wide = cols + 2 * reach
taps = 2 * reach + 1
basis = 3
points = rows * cols
hidden_units = 1024
chunk_rows = 2
chunk = chunk_rows * cols
chunks = rows // chunk_rows
span = basis * cols
depth = 3 * wide
f32 = jnp.float32
bf16 = jnp.bfloat16


def mm(a, b):
    return jnp.dot(a, b, preferred_element_type=f32)


def mm_nt(a, b):
    return lax.dot_general(a, b, (((1,), (1,)), ((), ())), preferred_element_type=f32)


def mm_tn(a, b):
    return lax.dot_general(a, b, (((0,), (0,)), ((), ())), preferred_element_type=f32)


class Halo:
    def __init__(self, place):
        lat, lon = place.lat, place.lon
        top = (lat == 0).astype(jnp.int32)
        bottom = (lat == 15).astype(jnp.int32)
        self.top, self.bottom = top, bottom
        self.lat, self.lon = lat, lon
        self.north = lat - 1 + top
        self.south = lat + 1 - bottom
        self.side_n = 1 - top
        self.side_s = bottom

    def upper(self, shift):
        return (self.north, lax.rem(self.lon + 16 + shift + 8 * self.top, 16))

    def lower(self, shift):
        return (self.south, lax.rem(self.lon + 16 + shift + 8 * self.bottom, 16))

    def beside(self, shift):
        return (self.lat, lax.rem(self.lon + 16 + shift, 16))

    def everyone(self):
        return [self.upper(s) for s in (0, -1, 1)] + [self.lower(s) for s in (0, -1, 1)] + [self.beside(-1), self.beside(1)]

    def send(self, ext, send, recv):
        own = slice(reach, reach + cols)
        first, last = slice(reach, 2 * reach), slice(cols, cols + reach)
        left, right = slice(0, reach), slice(reach + cols, wide)
        copies = []
        copies.append(remote(ext.at[1 : rows + 1, first], ext.at[1 : rows + 1, right], send.at[6], recv.at[6], self.beside(-1)))
        copies.append(remote(ext.at[1 : rows + 1, last], ext.at[1 : rows + 1, left], send.at[7], recv.at[7], self.beside(1)))
        for number, (side, target, row) in enumerate(((self.side_n, self.upper, 1), (self.side_s, self.lower, rows))):
            to = side * (rows + 1)
            plan = ((own, own, 0), (first, right, -1), (last, left, 1))
            for part, (src, dst, shift) in enumerate(plan):
                copies.append(
                    remote(
                        ext.at[row, src], ext.at[to, dst], send.at[number * 3 + part], recv.at[side * 3 + part], target(shift)
                    )
                )
        for copy in copies:
            copy.start()
        return copies

    def wait(self, ext, send, recv):
        own = slice(reach, reach + cols)
        left, right = slice(0, reach), slice(reach + cols, wide)
        me = self.beside(1)
        for side in range(2):
            for part, where in enumerate((own, right, left)):
                here = ext.at[side * (rows + 1), where]
                remote(here, here, send.at[0], recv.at[side * 3 + part], me).wait_recv()
        here = ext.at[1 : rows + 1, right]
        remote(here, here, send.at[0], recv.at[6], me).wait_recv()
        here = ext.at[1 : rows + 1, left]
        remote(here, here, send.at[0], recv.at[7], me).wait_recv()


def toeplitz(row):
    spread = jnp.broadcast_to(row, (cols, wide))
    return pltpu.roll(spread, 0, 1, stride=1, stride_axis=0).astype(bf16)


def step_kernel(
    scale,
    field_in, taps_in, mix_in, up_in, down_in, cot_in,
    block_out, field_out, mix_out, up_out, down_out,
    ext, gext, band, adjoint, tapx, feats, cot, hidden, act_grad, act, pre_grad, out_rows, mix, up, down,
    g_mlp, g_mix, t_mlp, t_mix,
    load_sem, store_sem, halo_send, halo_recv, grad_send, grad_recv, tap_send, tap_recv,
    *rest,
):
    place = Place()
    halo = Halo(place)
    own = slice(reach, reach + cols)

    loads = [
        pltpu.make_async_copy(taps_in, tapx.at[1 : rows + 1], load_sem.at[0]),
        pltpu.make_async_copy(field_in, ext.at[1 : rows + 1, own], load_sem.at[1]),
        pltpu.make_async_copy(cot_in, cot, load_sem.at[2]),
        pltpu.make_async_copy(down_in, down, load_sem.at[3]),
        pltpu.make_async_copy(mix_in, mix, load_sem.at[4]),
        pltpu.make_async_copy(up_in, up, load_sem.at[5]),
    ]
    for load in loads:
        load.start()
    devices = place.everyone() + halo.everyone()
    barrier = pltpu.get_barrier_semaphore()
    for device in devices:
        pl.semaphore_signal(barrier, inc=1, device_id=device, device_id_type=MESH)

    loads[0].wait()

    def build(r, carry):
        for k in range(basis):
            for d in range(3):
                band[r, k * cols : (k + 1) * cols, d * wide : (d + 1) * wide] = toeplitz(
                    tapx[r + 1, k * 3 + d : k * 3 + d + 1, :]
                )
        return carry

    lax.fori_loop(0, rows, build, 0)
    loads[1].wait()
    pl.semaphore_wait(barrier, len(devices))
    sent = halo.send(ext, halo_send, halo_recv)
    tap_copies = [
        remote(tapx.at[1], tapx.at[halo.side_n * (rows + 1)], tap_send.at[0], tap_recv.at[halo.side_n], halo.upper(0)),
        remote(tapx.at[rows], tapx.at[halo.side_s * (rows + 1)], tap_send.at[1], tap_recv.at[halo.side_s], halo.lower(0)),
    ]
    for copy in tap_copies:
        copy.start()
    sent += tap_copies

    loads[2].wait()
    loads[3].wait()

    def early(i, carry):
        at = pl.ds(multiple(i * chunk, 16), chunk)
        grad = cot[pl.ds(i * chunk_rows, chunk_rows)].reshape(chunk, lanes)
        act_grad[at, :] = mm_nt(grad, down[...])
        return carry

    lax.fori_loop(0, chunks, early, 0)

    def build_back(r, carry):
        for k in range(basis):
            for s in range(3):
                at = 9 + k * 3 + 2 - s
                adjoint[r, k * cols : (k + 1) * cols, s * wide : (s + 1) * wide] = toeplitz(tapx[r + s, at : at + 1, :])
        return carry

    lax.fori_loop(1, rows - 1, build_back, 0)

    loads[4].wait()
    loads[5].wait()
    halo.wait(ext, halo_send, halo_recv)

    def features(r, carry):
        window = ext[pl.ds(r, 3)].reshape(depth, lanes)
        made = mm(band[r], window).astype(bf16)
        at = pl.ds(multiple(r * cols, 16), cols)
        for k in range(basis):
            feats[k, at, :] = made[k * cols : (k + 1) * cols]
        return carry

    lax.fori_loop(0, rows, features, 0)

    def pointwise(i, carry):
        at = pl.ds(multiple(i * chunk, 16), chunk)
        total = ext[pl.ds(1 + i * chunk_rows, chunk_rows), own].reshape(chunk, lanes).astype(f32)
        for k in range(basis):
            total = total + mm(feats[k, at, :], mix[k])
        inner = total.astype(bf16)
        hidden[at, :] = inner
        for block in range(hidden_units // 256):
            f = slice(block * 256, (block + 1) * 256)
            value = mm(inner, up[:, f])
            cdf = 0.5 * (1.0 + lax.erf(value * inv_root_two))
            act[at, f] = (value * cdf).astype(bf16)
            slope = cdf + value * jnp.exp(-0.5 * value * value) * inv_root_tau
            pre_grad[at, f] = (act_grad[at, f] * slope).astype(bf16)
        made = (inner.astype(f32) + mm(act[at, :], down[...])).astype(bf16)
        out_rows[pl.ds(i * chunk_rows, chunk_rows)] = made.reshape(chunk_rows, cols, lanes)
        grad = cot[pl.ds(i * chunk_rows, chunk_rows)].reshape(chunk, lanes).astype(f32)
        grad = (grad + mm_nt(pre_grad[at, :], up[...])).astype(bf16)
        gext[pl.ds(1 + i * chunk_rows, chunk_rows), own] = grad.reshape(chunk_rows, cols, lanes)
        return carry

    lax.fori_loop(0, chunks, pointwise, 0)
    stores = [pltpu.make_async_copy(out_rows, block_out, store_sem.at[0])]
    stores[0].start()
    sent += halo.send(gext, grad_send, grad_recv)

    def flat(ref):
        return ref[...].reshape(points, lanes)

    def weight_down(i, carry):
        part = pl.ds(multiple(i * 256, 256), 256)
        g_mlp[pl.ds(multiple(1024 + i * 256, 256), 256), :] = mm_tn(act[:, part], flat(cot)).astype(bf16)
        return carry

    lax.fori_loop(0, 4, weight_down, 0)

    def weight_up(i, carry):
        part = pl.ds(multiple(i * 256, 256), 256)
        left = hidden[:, part]
        for side in range(2):
            g_mlp[pl.ds(multiple(side * 512 + i * 256, 256), 256), :] = mm_tn(
                left, pre_grad[:, side * 512 : side * 512 + 512]
            ).astype(bf16)
        return carry

    lax.fori_loop(0, 2, weight_up, 0)

    mlp_sum = Reduction(place, 2048, g_mlp, t_mlp, rest[0:8], rest[16], rest[17], scale)
    mix_sum = Reduction(place, 1536, g_mix, t_mix, rest[8:16], rest[18], rest[19], scale)
    mlp_sum.start_pair()

    def weight_mix(i, carry):
        k, half = lax.div(i, 2), lax.rem(i, 2)
        part = pl.ds(multiple(half * 256, 256), 256)
        grad = gext[1 : rows + 1, own].reshape(points, lanes)
        g_mix[pl.ds(multiple(i * 256, 256), 256), :] = mm_tn(feats[k, :, part], grad).astype(bf16)
        return carry

    lax.fori_loop(0, 6, weight_mix, 0)
    mix_sum.start_pair()
    mlp_sum.pair_then_first()

    for side in range(2):
        here = tapx.at[side * (rows + 1)]
        remote(here, here, tap_send.at[0], tap_recv.at[side], halo.beside(1)).wait_recv()
    for r, pole in ((0, halo.top), (rows - 1, halo.bottom)):
        for k in range(basis):
            for s in range(3):
                at = 9 + k * 3 + 2 - s
                row = tapx[r + s, at : at + 1, :]
                if (r, s) == (0, 0) or (r, s) == (rows - 1, 2):
                    other = 9 + k * 3 + s
                    row = jnp.where(pole == 1, tapx[r + s, other : other + 1, :], row)
                adjoint[r, k * cols : (k + 1) * cols, s * wide : (s + 1) * wide] = toeplitz(row)
    halo.wait(gext, grad_send, grad_recv)

    def pull(r, carry):
        window = gext[pl.ds(r, 3)].reshape(depth, lanes)
        made = mm(adjoint[r], window).astype(bf16)
        at = pl.ds(multiple(r * cols, 16), cols)
        for k in range(basis):
            feats[k, at, :] = made[k * cols : (k + 1) * cols]
        return carry

    lax.fori_loop(0, rows, pull, 0)
    mix_sum.pair_then_first()
    stores[0].wait()

    def last(i, carry):
        at = pl.ds(multiple(i * chunk, 16), chunk)
        total = gext[pl.ds(1 + i * chunk_rows, chunk_rows), own].reshape(chunk, lanes).astype(f32)
        for k in range(basis):
            total = total + mm_nt(feats[k, at, :], mix[k])
        out_rows[pl.ds(i * chunk_rows, chunk_rows)] = total.astype(bf16).reshape(chunk_rows, cols, lanes)
        return carry

    lax.fori_loop(0, chunks, last, 0)
    stores = [pltpu.make_async_copy(out_rows, field_out, store_sem.at[1])]
    stores[0].start()

    for stage in ("first_then_second", "second_then_z", "z_then_back", "back_second", "back_first", "back_pair", "finish"):
        for item in (mlp_sum, mix_sum):
            getattr(item, stage)()
    stores.append(pltpu.make_async_copy(t_mlp.at[0:512], up_out.at[:, 0:512], store_sem.at[2]))
    stores.append(pltpu.make_async_copy(t_mlp.at[512:1024], up_out.at[:, 512:1024], store_sem.at[3]))
    stores.append(pltpu.make_async_copy(t_mlp.at[1024:2048], down_out, store_sem.at[4]))
    for k in range(basis):
        stores.append(pltpu.make_async_copy(t_mix.at[k * 512 : k * 512 + 512], mix_out.at[k], store_sem.at[5 + k]))
    for store in stores[1:]:
        store.start()
    for store in stores:
        store.wait()
    for copy in sent:
        copy.wait_send()


def local(field_in, kernel_taps, row_reach, mix_weight, up_weight, down_weight, cotangent):
    offsets = jnp.arange(taps, dtype=jnp.int32) - reach
    mask = jnp.abs(offsets)[None, :] <= row_reach[:, None]
    masked = jnp.where(mask[None, :, None, :], kernel_taps, jnp.zeros((), kernel_taps.dtype)).astype(f32)
    masked = jnp.transpose(masked, (1, 0, 2, 3)).reshape(rows, 9, taps)
    tap_rows = jnp.concatenate([masked, masked[:, :, ::-1]], axis=1)
    tap_rows = jnp.pad(tap_rows, ((0, 0), (0, 6), (0, wide - taps)))
    total_points = points * lax.axis_size("lat") * lax.axis_size("lon")
    scale = 1.0 / math.sqrt(total_points)
    anywhere = pl.BlockSpec(memory_space=pl.ANY)
    v = pltpu.VMEM
    dma = pltpu.SemaphoreType.DMA
    return pl.pallas_call(
        lambda *refs: step_kernel(scale, *refs),
        out_shape=(
            jax.ShapeDtypeStruct(field_in.shape, bf16),
            jax.ShapeDtypeStruct(field_in.shape, bf16),
            jax.ShapeDtypeStruct(mix_weight.shape, bf16),
            jax.ShapeDtypeStruct(up_weight.shape, bf16),
            jax.ShapeDtypeStruct(down_weight.shape, bf16),
        ),
        in_specs=[anywhere] * 6,
        out_specs=(anywhere,) * 5,
        scratch_shapes=[
            v((rows + 2, wide, lanes), bf16),
            v((rows + 2, wide, lanes), bf16),
            v((rows, span, depth), bf16),
            v((rows, span, depth), bf16),
            v((rows + 2, 24, wide), f32),
            v((basis, points, lanes), bf16),
            v((rows, cols, lanes), bf16),
            v((points, lanes), bf16),
            v((points, hidden_units), f32),
            v((points, hidden_units), bf16),
            v((points, hidden_units), bf16),
            v((rows, cols, lanes), bf16),
            v((basis, lanes, lanes), bf16),
            v((lanes, hidden_units), bf16),
            v((hidden_units, lanes), bf16),
            v((2048, lanes), bf16),
            v((1536, lanes), bf16),
            v((2048, lanes), bf16),
            v((1536, lanes), bf16),
            dma((6,)), dma((8,)), dma((8,)), dma((8,)), dma((8,)), dma((8,)), dma((2,)), dma((2,)),
        ]
        + Reduction.scratch(2048)
        + Reduction.scratch(1536)
        + [dma((copies_each,)) for _ in range(4)],
        compiler_params=pltpu.CompilerParams(
            collective_id=0, has_side_effects=True, vmem_limit_bytes=64000 * 1024
        ),
        name="disco_step",
    )(field_in, tap_rows, mix_weight, up_weight, down_weight, cotangent)


def solution(mesh):
    placed = (
        P("lat", "lon", None),
        P(None, "lat", None, None),
        P("lat"),
        P(),
        P(),
        P(),
        P("lat", "lon", None),
    )
    return jax.shard_map(
        local,
        mesh=mesh,
        in_specs=placed,
        out_specs=(P("lat", "lon", None), P("lat", "lon", None), P(), P(), P()),
        check_vma=False,
    )
```

time: 158 us -> 94.7 us (0.60)
  waiting for transfers between devices: 30.2 us -> 0 us
  matrix products: 27.5 us -> 0 us
  Pallas kernels: 60.7 us -> 83.8 us
  starting transfers between devices: 20.7 us -> 0 us
  other arithmetic: 6.91 us -> 2.18 us
  local copies, waits for them, and re-layouts: 9.6 us -> 7.77 us
    ppermute x10 -> x0, waiting for transfers between devices: 30.2 us -> none  [the longest x4 11.5 us: extended_2(): after = lax.ppermute(leading, axis, down)]
    dot_general x12 -> x0, matrix products: 27.5 us -> none  [the longest x1 4.12 us: local(): pre_act = jnp.dot(hidden, up_weight, preferred_element_type=jnp.float32)]
    pallas_call x1, Pallas kernels: 60.7 us -> 83.8 us  [local(): pl.pallas_call(lambda *refs: step_kernel(scale, *refs), out_shape=(jax.Sh...]
    ppermute x10 -> x0, starting transfers between devices: 20.7 us -> none  [the longest x4 14.1 us: extended_2(): before = lax.ppermute(last, axis, up)]
    unnamed x39 -> x13, local copies, waits for them, and re-layouts: 3.56 us -> 7.68 us
    slice x11 -> x0, local copies, waits for them, and re-layouts: 3.96 us -> none  [the longest x1 2.26 us: local(): down_out = mlp_out[2 * channels:]]
    concatenate x3 -> x1, other arithmetic: 2.7 us -> 0.68 us  [local(): tap_rows = jnp.concatenate([masked, masked[:, :, ::-1]], axis=1)]
    another operation x5 -> x0, other arithmetic: 1.65 us -> none
  transfers between devices with their start and end apart: 10 -> 0, of which waited for: 8 -> 0; matrix products, arithmetic and copies ran while one was open for 4% -> 0% of each run, Pallas kernels for 0% -> 0%
where the time goes in v2:
time: 94.7 us; the launch traced here: 94.5 us
  Pallas kernels  83.8 us (88%)
  local copies, waits for them, and re-layouts  7.77 us (8%)
  other arithmetic  2.18 us (2%)
    pallas_call x1, Pallas kernels, local(): pl.pallas_call(lambda *refs: step_kernel(scale, *refs), out_shape=(jax.Sh...  83.8 us
    unnamed x13, local copies, waits for them, and re-layouts  7.68 us

profile of v2, /device:TPU:1, one launch (start us, length us, event | category | flops | bytes accessed | tf_op | source)
XLA Modules:
  0.0 94.5 jit_solution(12239023348667142499)
XLA Ops:
  0.6 0.7 broadcast_compare_fusion
  1.4 0.8 fusion
  2.2 0.1 rev.3
  2.3 0.7 select_maximum_fusion.refs_1_
  2.9 83.8 %disco_step.1 = (bf16[10,96,512]{2,1,0:T(8,128)(2,1)}, bf16[10,96,512]{2,1,0:T(8,128)(2,1)}, bf16[3,512,512]{2,1,0:T(8,128)(2,1)}, bf16[512,1024]{1,0:T(8,128)(2,1)}, bf16[1024,512]{1,0:T(8,128)(2,1)}) custom-call(bf16[10,96,512]{2,1,0:T(8,128)(2,1)} %refs_0_.1, f32[10,24,128]{2,1,0:T(8,128)} %select_maximum_fusion.refs_1_, bf16[3,512,512]{2,1,0:T(8,128)(2,1)} %refs_2_.1, ...), custom_call_target="tpu_custom_call" | custom-call | tf_op jit(solution)/shard_map/disco_step/pallas_call | solution.py:514
  86.8 0.0 copy-start.3
  86.8 0.0 copy-start
  86.8 2.4 %copy.24 = bf16[10,96,512]{2,1,0:T(8,128)(2,1)} copy(bf16[10,96,512]{2,1,0:T(8,128)(2,1)} %get-tuple-element.10) | data formatting | bytes 1966080
  89.2 0.0 copy-done.3
  89.2 0.9 copy.25
  90.1 0.0 copy-done
  90.1 0.0 copy-start.2
  90.1 1.1 %copy.26 = bf16[3,512,512]{2,1,0:T(8,128)(2,1)} copy(bf16[3,512,512]{2,1,0:T(8,128)(2,1)S(1)} %copy-done) | data formatting | bytes 3145728
  91.3 0.6 copy-done.2
  91.9 0.0 copy-start.1
  91.9 1.0 %copy.27 = bf16[512,1024]{1,0:T(8,128)(2,1)} copy(bf16[512,1024]{1,0:T(8,128)(2,1)S(1)} %copy-done.2) | data formatting | bytes 2097152
  92.9 0.6 copy-done.1
  93.5 1.0 %copy.28 = bf16[1024,512]{1,0:T(8,128)(2,1)} copy(bf16[1024,512]{1,0:T(8,128)(2,1)S(1)} %copy-done.1) | data formatting | bytes 2097152
  (2 shorter events, 0.0 us)
Async XLA Ops:
  86.8 2.4 %copy-start.3 = (bf16[10,96,512]{2,1,0:T(8,128)(2,1)S(1)}, bf16[10,96,512]{2,1,0:T(8,128)(2,1)}, u32[]{:S(2)}) copy-start(bf16[10,96,512]{2,1,0:T(8,128)(2,1)} %get-tuple-element.11) | copy-start | bytes 2949124
  86.8 3.3 %copy-start = (bf16[3,512,512]{2,1,0:T(8,128)(2,1)S(1)}, bf16[3,512,512]{2,1,0:T(8,128)(2,1)}, u32[]{:S(2)}) copy-start(bf16[3,512,512]{2,1,0:T(8,128)(2,1)} %get-tuple-element.12) | copy-start | bytes 4718596
  90.1 1.8 %copy-start.2 = (bf16[512,1024]{1,0:T(8,128)(2,1)S(1)}, bf16[512,1024]{1,0:T(8,128)(2,1)}, u32[]{:S(2)}) copy-start(bf16[512,1024]{1,0:T(8,128)(2,1)} %get-tuple-element.13) | copy-start | bytes 3145732
  91.9 1.6 %copy-start.1 = (bf16[1024,512]{1,0:T(8,128)(2,1)S(1)}, bf16[1024,512]{1,0:T(8,128)(2,1)}, u32[]{:S(2)}) copy-start(bf16[1024,512]{1,0:T(8,128)(2,1)} %get-tuple-element.14) | copy-start | bytes 3145732

commit v3 on v2

--- a/solution.py
+++ b/solution.py
@@ -87,11 +87,10 @@
 
 
 class Reduction:
-    def __init__(self, place, rows, grad, out, parts, send, recv, scale):
+    def __init__(self, place, start, rows, grad, out, parts, send, recv, scale):
         self.p = place
-        self.rows = rows
         self.half, self.quarter, self.piece = rows // 2, rows // 8, rows // 32
-        self.grad, self.out, self.scale = grad, out, scale
+        self.grad, self.out, self.scale = grad.at[start : start + rows], out.at[start : start + rows], scale
         self.r0, self.s0, self.r1, self.s1, self.r2, self.s2, self.r3, self.zbuf = parts
         self.send, self.recv = send, recv
         self.used = 0
@@ -102,7 +101,7 @@
         half, quarter, piece = rows // 2, rows // 8, rows // 32
         shapes = [
             (half, lanes), (half, lanes), (3, quarter, lanes), (quarter, lanes),
-            (3, piece, lanes), (64, lanes), (7, 16, 256), (64, lanes),
+            (3, piece, lanes), (32, lanes), (7, 16, 128), (32, lanes),
         ]
         return [pltpu.VMEM(s, jnp.bfloat16) for s in shapes]
 
@@ -150,17 +149,17 @@
         self.flight = flight
 
     def spot(self, ref, index):
-        row = multiple(lax.div(index, 2) * 16, 16)
-        lane = multiple(lax.rem(index, 2) * 256, 256)
-        return ref.at[pl.ds(row, 16), pl.ds(lane, 256)]
+        row = multiple(lax.div(index, 4) * 16, 16)
+        lane = multiple(lax.rem(index, 4) * 128, 128)
+        return ref.at[pl.ds(row, 16), pl.ds(lane, 128)]
 
     def second_then_z(self):
         p = self.p
         self.arrived()
         sources = [(self.s1, p.second * self.piece)] + [(self.r2.at[i], 0) for i in range(3)]
         add_rows(self.s2, 0, sources, self.piece, 16)
-        if self.piece < 64:
-            self.s2[self.piece :, :] = jnp.zeros((64 - self.piece, lanes), jnp.bfloat16)
+        if self.piece < 32:
+            self.s2[self.piece :, :] = jnp.zeros((32 - self.piece, lanes), jnp.bfloat16)
         flight = []
         for step in z_steps:
             src = self.spot(self.s2, lax.rem(p.z + step, ring_z))
@@ -205,11 +204,13 @@
 
 
 copies_each = 28
+stacks = ((0, 1024), (1024, 1024), (2048, 1024), (3072, 512))
 
 
 rows = 10
 cols = 96
 reach = 16
+vmem_room = 48 * 1024 * 1024
 wide = cols + 2 * reach
 taps = 2 * reach + 1
 basis = 3
@@ -280,7 +281,13 @@
             copy.start()
         return copies
 
-    def wait(self, ext, send, recv):
+    def wait_columns(self, ext, send, recv):
+        me = self.beside(1)
+        for number, first in ((6, reach + cols), (7, 0)):
+            here = ext.at[1 : rows + 1, first : first + reach]
+            remote(here, here, send.at[0], recv.at[number], me).wait_recv()
+
+    def wait_rows(self, ext, send, recv):
         own = slice(reach, reach + cols)
         left, right = slice(0, reach), slice(reach + cols, wide)
         me = self.beside(1)
@@ -288,10 +295,6 @@
             for part, where in enumerate((own, right, left)):
                 here = ext.at[side * (rows + 1), where]
                 remote(here, here, send.at[0], recv.at[side * 3 + part], me).wait_recv()
-        here = ext.at[1 : rows + 1, right]
-        remote(here, here, send.at[0], recv.at[6], me).wait_recv()
-        here = ext.at[1 : rows + 1, left]
-        remote(here, here, send.at[0], recv.at[7], me).wait_recv()
 
 
 def toeplitz(row):
@@ -302,10 +305,10 @@
 def step_kernel(
     scale,
     field_in, taps_in, mix_in, up_in, down_in, cot_in,
-    block_out, field_out, mix_out, up_out, down_out,
-    ext, gext, band, adjoint, tapx, feats, cot, hidden, act_grad, act, pre_grad, out_rows, mix, up, down,
-    g_mlp, g_mix, t_mlp, t_mix,
-    load_sem, store_sem, halo_send, halo_recv, grad_send, grad_recv, tap_send, tap_recv,
+    block_rows, field_rows, total,
+    ext, gext, band, adjoint, tapx, revx, feats, cot, hidden, act_grad, act, pre_grad, mix, up, down,
+    grads,
+    load_sem, halo_send, halo_recv, grad_send, grad_recv, tap_send, tap_recv,
     *rest,
 ):
     place = Place()
@@ -313,7 +316,7 @@
     own = slice(reach, reach + cols)
 
     loads = [
-        pltpu.make_async_copy(taps_in, tapx.at[1 : rows + 1], load_sem.at[0]),
+        pltpu.make_async_copy(taps_in, tapx.at[:, 1 : rows + 1], load_sem.at[0]),
         pltpu.make_async_copy(field_in, ext.at[1 : rows + 1, own], load_sem.at[1]),
         pltpu.make_async_copy(cot_in, cot, load_sem.at[2]),
         pltpu.make_async_copy(down_in, down, load_sem.at[3]),
@@ -333,7 +336,7 @@
         for k in range(basis):
             for d in range(3):
                 band[r, k * cols : (k + 1) * cols, d * wide : (d + 1) * wide] = toeplitz(
-                    tapx[r + 1, k * 3 + d : k * 3 + d + 1, :]
+                    tapx[k, r + 1, d : d + 1, :]
                 )
         return carry
 
@@ -342,8 +345,8 @@
     pl.semaphore_wait(barrier, len(devices))
     sent = halo.send(ext, halo_send, halo_recv)
     tap_copies = [
-        remote(tapx.at[1], tapx.at[halo.side_n * (rows + 1)], tap_send.at[0], tap_recv.at[halo.side_n], halo.upper(0)),
-        remote(tapx.at[rows], tapx.at[halo.side_s * (rows + 1)], tap_send.at[1], tap_recv.at[halo.side_s], halo.lower(0)),
+        remote(tapx.at[:, 1], tapx.at[:, halo.side_n * (rows + 1)], tap_send.at[0], tap_recv.at[halo.side_n], halo.upper(0)),
+        remote(tapx.at[:, rows], tapx.at[:, halo.side_s * (rows + 1)], tap_send.at[1], tap_recv.at[halo.side_s], halo.lower(0)),
     ]
     for copy in tap_copies:
         copy.start()
@@ -360,18 +363,22 @@
 
     lax.fori_loop(0, chunks, early, 0)
 
+    row_at = lax.broadcasted_iota(jnp.int32, (wide, wide), 0)
+    mirror = (row_at + lax.broadcasted_iota(jnp.int32, (wide, wide), 1) == taps - 1).astype(f32).astype(bf16)
+    straight = tapx[:, 1 : rows + 1].reshape(basis * rows * 8, wide).astype(bf16)
+    revx[:, 1 : rows + 1] = mm(straight, mirror).reshape(basis, rows, 8, wide)
+
     def build_back(r, carry):
         for k in range(basis):
             for s in range(3):
-                at = 9 + k * 3 + 2 - s
-                adjoint[r, k * cols : (k + 1) * cols, s * wide : (s + 1) * wide] = toeplitz(tapx[r + s, at : at + 1, :])
+                adjoint[r, k * cols : (k + 1) * cols, s * wide : (s + 1) * wide] = toeplitz(revx[k, r + s, 2 - s : 3 - s, :])
         return carry
 
     lax.fori_loop(1, rows - 1, build_back, 0)
 
     loads[4].wait()
     loads[5].wait()
-    halo.wait(ext, halo_send, halo_recv)
+    halo.wait_columns(ext, halo_send, halo_recv)
 
     def features(r, carry):
         window = ext[pl.ds(r, 3)].reshape(depth, lanes)
@@ -381,7 +388,10 @@
             feats[k, at, :] = made[k * cols : (k + 1) * cols]
         return carry
 
-    lax.fori_loop(0, rows, features, 0)
+    lax.fori_loop(1, rows - 1, features, 0)
+    halo.wait_rows(ext, halo_send, halo_recv)
+    features(0, 0)
+    features(rows - 1, 0)
 
     def pointwise(i, carry):
         at = pl.ds(multiple(i * chunk, 16), chunk)
@@ -398,66 +408,72 @@
             slope = cdf + value * jnp.exp(-0.5 * value * value) * inv_root_tau
             pre_grad[at, f] = (act_grad[at, f] * slope).astype(bf16)
         made = (inner.astype(f32) + mm(act[at, :], down[...])).astype(bf16)
-        out_rows[pl.ds(i * chunk_rows, chunk_rows)] = made.reshape(chunk_rows, cols, lanes)
+        block_rows[pl.ds(i * chunk_rows, chunk_rows)] = made.reshape(chunk_rows, cols, lanes)
         grad = cot[pl.ds(i * chunk_rows, chunk_rows)].reshape(chunk, lanes).astype(f32)
         grad = (grad + mm_nt(pre_grad[at, :], up[...])).astype(bf16)
         gext[pl.ds(1 + i * chunk_rows, chunk_rows), own] = grad.reshape(chunk_rows, cols, lanes)
         return carry
 
     lax.fori_loop(0, chunks, pointwise, 0)
-    stores = [pltpu.make_async_copy(out_rows, block_out, store_sem.at[0])]
-    stores[0].start()
     sent += halo.send(gext, grad_send, grad_recv)
 
     def flat(ref):
         return ref[...].reshape(points, lanes)
 
+    sums = [
+        Reduction(place, start, count, grads, total, rest[8 * n : 8 * n + 8], rest[32 + 2 * n], rest[33 + 2 * n], scale)
+        for n, (start, count) in enumerate(stacks)
+    ]
+    sum_up, sum_down, sum_mix, sum_rest = sums
+
     def weight_down(i, carry):
         part = pl.ds(multiple(i * 256, 256), 256)
-        g_mlp[pl.ds(multiple(1024 + i * 256, 256), 256), :] = mm_tn(act[:, part], flat(cot)).astype(bf16)
+        grads[pl.ds(multiple(1024 + i * 256, 256), 256), :] = mm_tn(act[:, part], flat(cot)).astype(bf16)
         return carry
 
     lax.fori_loop(0, 4, weight_down, 0)
+    sum_down.start_pair()
 
     def weight_up(i, carry):
         part = pl.ds(multiple(i * 256, 256), 256)
         left = hidden[:, part]
         for side in range(2):
-            g_mlp[pl.ds(multiple(side * 512 + i * 256, 256), 256), :] = mm_tn(
+            grads[pl.ds(multiple(side * 512 + i * 256, 256), 256), :] = mm_tn(
                 left, pre_grad[:, side * 512 : side * 512 + 512]
             ).astype(bf16)
         return carry
 
     lax.fori_loop(0, 2, weight_up, 0)
-
-    mlp_sum = Reduction(place, 2048, g_mlp, t_mlp, rest[0:8], rest[16], rest[17], scale)
-    mix_sum = Reduction(place, 1536, g_mix, t_mix, rest[8:16], rest[18], rest[19], scale)
-    mlp_sum.start_pair()
+    sum_up.start_pair()
+    sum_down.pair_then_first()
 
     def weight_mix(i, carry):
         k, half = lax.div(i, 2), lax.rem(i, 2)
         part = pl.ds(multiple(half * 256, 256), 256)
         grad = gext[1 : rows + 1, own].reshape(points, lanes)
-        g_mix[pl.ds(multiple(i * 256, 256), 256), :] = mm_tn(feats[k, :, part], grad).astype(bf16)
-        return carry
-
-    lax.fori_loop(0, 6, weight_mix, 0)
-    mix_sum.start_pair()
-    mlp_sum.pair_then_first()
+        grads[pl.ds(multiple(2048 + i * 256, 256), 256), :] = mm_tn(feats[k, :, part], grad).astype(bf16)
+        return carry
+
+    lax.fori_loop(0, 4, weight_mix, 0)
+    sum_mix.start_pair()
+    sum_up.pair_then_first()
+    lax.fori_loop(4, 6, weight_mix, 0)
+    sum_rest.start_pair()
+    sum_mix.pair_then_first()
 
     for side in range(2):
-        here = tapx.at[side * (rows + 1)]
+        here = tapx.at[:, side * (rows + 1)]
         remote(here, here, tap_send.at[0], tap_recv.at[side], halo.beside(1)).wait_recv()
     for r, pole in ((0, halo.top), (rows - 1, halo.bottom)):
+        slot = 0 if r == 0 else rows + 1
+        straight = tapx[:, slot].reshape(basis * 8, wide).astype(bf16)
+        revx[:, slot] = mm(straight, mirror).reshape(basis, 8, wide)
         for k in range(basis):
             for s in range(3):
-                at = 9 + k * 3 + 2 - s
-                row = tapx[r + s, at : at + 1, :]
-                if (r, s) == (0, 0) or (r, s) == (rows - 1, 2):
-                    other = 9 + k * 3 + s
-                    row = jnp.where(pole == 1, tapx[r + s, other : other + 1, :], row)
+                row = revx[k, r + s, 2 - s : 3 - s, :]
+                if r + s == slot:
+                    row = jnp.where(pole == 1, revx[k, r + s, s : s + 1, :], row)
                 adjoint[r, k * cols : (k + 1) * cols, s * wide : (s + 1) * wide] = toeplitz(row)
-    halo.wait(gext, grad_send, grad_recv)
 
     def pull(r, carry):
         window = gext[pl.ds(r, 3)].reshape(depth, lanes)
@@ -467,91 +483,117 @@
             feats[k, at, :] = made[k * cols : (k + 1) * cols]
         return carry
 
-    lax.fori_loop(0, rows, pull, 0)
-    mix_sum.pair_then_first()
-    stores[0].wait()
+    halo.wait_columns(gext, grad_send, grad_recv)
+    lax.fori_loop(1, rows // 2, pull, 0)
+    sum_rest.pair_then_first()
+    lax.fori_loop(rows // 2, rows - 1, pull, 0)
+    halo.wait_rows(gext, grad_send, grad_recv)
+    pull(0, 0)
+    pull(rows - 1, 0)
+    sum_down.first_then_second()
 
     def last(i, carry):
         at = pl.ds(multiple(i * chunk, 16), chunk)
-        total = gext[pl.ds(1 + i * chunk_rows, chunk_rows), own].reshape(chunk, lanes).astype(f32)
+        made = gext[pl.ds(1 + i * chunk_rows, chunk_rows), own].reshape(chunk, lanes).astype(f32)
         for k in range(basis):
-            total = total + mm_nt(feats[k, at, :], mix[k])
-        out_rows[pl.ds(i * chunk_rows, chunk_rows)] = total.astype(bf16).reshape(chunk_rows, cols, lanes)
-        return carry
-
-    lax.fori_loop(0, chunks, last, 0)
-    stores = [pltpu.make_async_copy(out_rows, field_out, store_sem.at[1])]
-    stores[0].start()
-
-    for stage in ("first_then_second", "second_then_z", "z_then_back", "back_second", "back_first", "back_pair", "finish"):
-        for item in (mlp_sum, mix_sum):
-            getattr(item, stage)()
-    stores.append(pltpu.make_async_copy(t_mlp.at[0:512], up_out.at[:, 0:512], store_sem.at[2]))
-    stores.append(pltpu.make_async_copy(t_mlp.at[512:1024], up_out.at[:, 512:1024], store_sem.at[3]))
-    stores.append(pltpu.make_async_copy(t_mlp.at[1024:2048], down_out, store_sem.at[4]))
-    for k in range(basis):
-        stores.append(pltpu.make_async_copy(t_mix.at[k * 512 : k * 512 + 512], mix_out.at[k], store_sem.at[5 + k]))
-    for store in stores[1:]:
-        store.start()
-    for store in stores:
-        store.wait()
+            made = made + mm_nt(feats[k, at, :], mix[k])
+        field_rows[pl.ds(i * chunk_rows, chunk_rows)] = made.astype(bf16).reshape(chunk_rows, cols, lanes)
+        return carry
+
+    lax.fori_loop(0, 2, last, 0)
+    sum_up.first_then_second()
+    sum_down.second_then_z()
+    lax.fori_loop(2, chunks, last, 0)
+    stages = ("first_then_second", "second_then_z", "z_then_back", "back_second", "back_first", "back_pair", "finish")
+    order = (sum_down, sum_up, sum_mix, sum_rest)
+    done = {sum_down: 2, sum_up: 1, sum_mix: 0, sum_rest: 0}
+    for wave in range(2, len(stages) + len(order)):
+        for number in range(len(order)):
+            item, stage = order[number], wave - number
+            if done[item] <= stage < len(stages):
+                getattr(item, stages[stage])()
     for copy in sent:
         copy.wait_send()
 
 
 def local(field_in, kernel_taps, row_reach, mix_weight, up_weight, down_weight, cotangent):
-    offsets = jnp.arange(taps, dtype=jnp.int32) - reach
+    offsets = jnp.arange(wide, dtype=jnp.int32) - reach
     mask = jnp.abs(offsets)[None, :] <= row_reach[:, None]
-    masked = jnp.where(mask[None, :, None, :], kernel_taps, jnp.zeros((), kernel_taps.dtype)).astype(f32)
-    masked = jnp.transpose(masked, (1, 0, 2, 3)).reshape(rows, 9, taps)
-    tap_rows = jnp.concatenate([masked, masked[:, :, ::-1]], axis=1)
-    tap_rows = jnp.pad(tap_rows, ((0, 0), (0, 6), (0, wide - taps)))
+    tap_rows = jnp.pad(kernel_taps, ((0, 0), (0, 0), (0, 5), (0, wide - taps))).astype(f32)
+    tap_rows = jnp.where(mask[None, :, None, :], tap_rows, 0.0)
     total_points = points * lax.axis_size("lat") * lax.axis_size("lon")
     scale = 1.0 / math.sqrt(total_points)
     anywhere = pl.BlockSpec(memory_space=pl.ANY)
     v = pltpu.VMEM
     dma = pltpu.SemaphoreType.DMA
-    return pl.pallas_call(
+    resident = pl.BlockSpec(memory_space=pltpu.VMEM)
+    shape = jax.ShapeDtypeStruct
+    made = pl.pallas_call(
         lambda *refs: step_kernel(scale, *refs),
         out_shape=(
-            jax.ShapeDtypeStruct(field_in.shape, bf16),
-            jax.ShapeDtypeStruct(field_in.shape, bf16),
-            jax.ShapeDtypeStruct(mix_weight.shape, bf16),
-            jax.ShapeDtypeStruct(up_weight.shape, bf16),
-            jax.ShapeDtypeStruct(down_weight.shape, bf16),
+            shape(field_in.shape, bf16), shape(field_in.shape, bf16), shape((3584, lanes), bf16),
         ),
         in_specs=[anywhere] * 6,
-        out_specs=(anywhere,) * 5,
+        out_specs=(resident,) * 3,
         scratch_shapes=[
             v((rows + 2, wide, lanes), bf16),
             v((rows + 2, wide, lanes), bf16),
             v((rows, span, depth), bf16),
             v((rows, span, depth), bf16),
-            v((rows + 2, 24, wide), f32),
+            v((basis, rows + 2, 8, wide), f32),
+            v((basis, rows + 2, 8, wide), f32),
             v((basis, points, lanes), bf16),
             v((rows, cols, lanes), bf16),
             v((points, lanes), bf16),
             v((points, hidden_units), f32),
             v((points, hidden_units), bf16),
             v((points, hidden_units), bf16),
-            v((rows, cols, lanes), bf16),
             v((basis, lanes, lanes), bf16),
             v((lanes, hidden_units), bf16),
             v((hidden_units, lanes), bf16),
-            v((2048, lanes), bf16),
-            v((1536, lanes), bf16),
-            v((2048, lanes), bf16),
-            v((1536, lanes), bf16),
-            dma((6,)), dma((8,)), dma((8,)), dma((8,)), dma((8,)), dma((8,)), dma((2,)), dma((2,)),
+            v((3584, lanes), bf16),
+            dma((6,)), dma((8,)), dma((8,)), dma((8,)), dma((8,)), dma((2,)), dma((2,)),
         ]
-        + Reduction.scratch(2048)
-        + Reduction.scratch(1536)
-        + [dma((copies_each,)) for _ in range(4)],
+        + [part for start, count in stacks for part in Reduction.scratch(count)]
+        + [dma((copies_each,)) for _ in range(2 * len(stacks))],
         compiler_params=pltpu.CompilerParams(
-            collective_id=0, has_side_effects=True, vmem_limit_bytes=64000 * 1024
+            collective_id=0, has_side_effects=True, vmem_limit_bytes=vmem_room
         ),
         name="disco_step",
-    )(field_in, tap_rows, mix_weight, up_weight, down_weight, cotangent)
+    )(*[pltpu.with_memory_space_constraint(x, pltpu.HBM) for x in (field_in, tap_rows, mix_weight, up_weight, down_weight, cotangent)])
+    return store_all(*[pltpu.with_memory_space_constraint(x, pltpu.VMEM) for x in made])
+
+
+def store_kernel(block_rows, field_rows, total, block_out, field_out, mix_out, up_out, down_out, sem):
+    stores = [
+        pltpu.make_async_copy(block_rows, block_out, sem.at[0]),
+        pltpu.make_async_copy(field_rows, field_out, sem.at[1]),
+        pltpu.make_async_copy(total.at[0:512], up_out.at[:, 0:512], sem.at[2]),
+        pltpu.make_async_copy(total.at[512:1024], up_out.at[:, 512:1024], sem.at[3]),
+        pltpu.make_async_copy(total.at[1024:2048], down_out, sem.at[4]),
+    ]
+    for k in range(basis):
+        stores.append(pltpu.make_async_copy(total.at[2048 + k * 512 : 2560 + k * 512], mix_out.at[k], sem.at[5 + k]))
+    for store in stores:
+        store.start()
+    for store in stores:
+        store.wait()
+
+
+def store_all(block_rows, field_rows, total):
+    shape = jax.ShapeDtypeStruct
+    return pl.pallas_call(
+        store_kernel,
+        out_shape=(
+            shape(block_rows.shape, bf16), shape(field_rows.shape, bf16), shape((basis, lanes, lanes), bf16),
+            shape((lanes, hidden_units), bf16), shape((hidden_units, lanes), bf16),
+        ),
+        in_specs=[pl.BlockSpec(memory_space=pltpu.VMEM)] * 3,
+        out_specs=(pl.BlockSpec(memory_space=pltpu.HBM),) * 5,
+        scratch_shapes=[pltpu.SemaphoreType.DMA((8,))],
+        compiler_params=pltpu.CompilerParams(vmem_limit_bytes=1024 * 1024),
+        name="store_all",
+    )(block_rows, field_rows, total)
 
 
 def solution(mesh):

time: 94.7 us -> 92.5 us (0.977)
  local copies, waits for them, and re-layouts: 7.77 us -> 0 us
  Pallas kernels: 83.8 us -> 89.5 us
    unnamed x13 -> x0, local copies, waits for them, and re-layouts: 7.68 us -> none
    pallas_call x1 -> x2, Pallas kernels: 83.8 us -> 89.5 us  [the longest x1 87 us: local(): pl.pallas_call(lambda *refs: step_kernel(scale, *refs), out_shape=(shape(...]
    select_n x0 -> x1, other arithmetic: none -> 1.42 us  [local(): tap_rows = jnp.where(mask[None, :, None, :], tap_rows, 0.0)]
where the time goes in v3:
time: 92.5 us; the launch traced here: 92.3 us
  Pallas kernels  89.5 us (97%)
  other arithmetic  2.16 us (2%)
    pallas_call x1, Pallas kernels, local(): pl.pallas_call(lambda *refs: step_kernel(scale, *refs), out_shape=(shape(...  87 us
    pallas_call x1, Pallas kernels, store_all(): pl.pallas_call(store_kernel, out_shape=(shape(block_rows.shape, bf16), sh...  2.53 us

profile of v3, /device:TPU:1, one launch (start us, length us, event | category | flops | bytes accessed | tf_op | source)
XLA Modules:
  0.0 92.3 jit_solution(16686789241072884302)
XLA Ops:
  0.6 0.7 broadcast_compare_fusion
  1.4 1.4 %convert_select_fusion.refs_1_ = f32[3,10,8,128]{3,2,1,0:T(8,128)} fusion(bf16[3,10,3,33]{3,2,1,0:T(4,128)(2,1)} %param.8, pred[10,128]{1,0:T(8,128)(4,1)S(1)} %broadcast_compare_fusion), kind=kLoop, calls=%fused_computation | loop fusion | flops 61440 | bytes 130100 | tf_op jit(solution)/shard_map/jit(_where)/select_n | solution.py:523
  2.8 87.0 %disco_step.1 = (bf16[10,96,512]{2,1,0:T(8,128)(2,1)S(1)}, bf16[10,96,512]{2,1,0:T(8,128)(2,1)S(1)}, bf16[3584,512]{1,0:T(8,128)(2,1)S(1)}) custom-call(bf16[10,96,512]{2,1,0:T(8,128)(2,1)} %refs_0_.1, f32[3,10,8,128]{3,2,1,0:T(8,128)} %convert_select_fusion.refs_1_, bf16[3,512,512]{2,1,0:T(8,128)(2,1)} %refs_2_.1, bf16[512,1024]{1,0:T(8,128)(2,1)} %refs_3_.1, ...), custom_call_target="tpu_custom_call" | custom-call | tf_op jit(solution)/shard_map/disco_step/pallas_call | solution.py:531
  89.8 2.5 %store_all.1 = (bf16[10,96,512]{2,1,0:T(8,128)(2,1)}, bf16[10,96,512]{2,1,0:T(8,128)(2,1)}, bf16[3,512,512]{2,1,0:T(8,128)(2,1)}, bf16[512,1024]{1,0:T(8,128)(2,1)}, bf16[1024,512]{1,0:T(8,128)(2,1)}) custom-call(bf16[10,96,512]{2,1,0:T(8,128)(2,1)S(1)} %get-tuple-element.8.block_rows, bf16[10,96,512]{2,1,0:T(8,128)(2,1)S(1)} %get-tuple-element.9.field_rows, ...), custom_call_target="tpu_custom_call" | custom-call | tf_op jit(solution)/shard_map/store_all/pallas_call | solution.py:585
  (1 shorter events, 0.0 us)

commit v4 on v3

--- a/solution.py
+++ b/solution.py
@@ -122,17 +122,42 @@
             copy.wait_recv()
         self.flight = []
 
+    def block(self, ref, index, part):
+        half = self.quarter // 2
+        return ref.at[pl.ds(multiple(index * self.quarter + part * half, 16), half), :]
+
     def pair_then_first(self):
         p = self.p
         self.arrived()
-        flight = []
-        for step in (2, 1, 3, 0):
-            at = lax.rem(p.first + step, ring_xy) * self.quarter
-            add_rows(self.s0, at, [(self.grad, p.core * self.half + at), (self.r0, at)], self.quarter, 32)
-            if step:
-                src = self.s0.at[pl.ds(multiple(at, 16), self.quarter), :]
-                flight.append(self.go(src, self.r1.at[step - 1], p.along_first(step)))
-        self.flight = flight
+        half = self.quarter // 2
+        place = [lax.rem(p.first + step, ring_xy) for step in range(ring_xy)]
+
+        def join(step):
+            at = place[step] * self.quarter
+            add_rows(self.s0, at, [(self.grad, p.core * self.half + at), (self.r0, at)], self.quarter, 64)
+
+        top, low = self.r1.at[2, 0:half], self.r1.at[2, half : 2 * half]
+        join(2)
+        self.relayed = [
+            self.go(self.block(self.s0, place[2], 0), top, p.along_first(1)),
+            self.go(self.block(self.s0, place[2], 1), low, p.along_first(3)),
+        ]
+        join(1)
+        self.flight = [self.go(self.block(self.s0, place[1], 1), self.r1.at[0, half : 2 * half], p.along_first(1))]
+        join(3)
+        self.flight.append(self.go(self.block(self.s0, place[3], 0), self.r1.at[1, 0:half], p.along_first(3)))
+        join(0)
+
+    def first_relay(self):
+        p = self.p
+        half = self.quarter // 2
+        for copy, step, part in ((self.relayed[0], 1, 0), (self.relayed[1], 3, 1)):
+            copy.wait_recv()
+            index = lax.rem(p.first + step, ring_xy)
+            at = index * self.quarter + part * half
+            add_rows(self.s0, at, [(self.s0, at), (self.r1.at[2], part * half)], half, half)
+            land = self.r1.at[0 if step == 1 else 1, part * half : part * half + half]
+            self.flight.append(self.go(self.block(self.s0, index, part), land, p.along_first(step)))
 
     def first_then_second(self):
         p = self.p
@@ -141,7 +166,7 @@
         own = p.first * self.quarter
         for step in (2, 1, 3, 0):
             at = lax.rem(p.second + step, ring_xy) * self.piece
-            sources = [(self.s0, own + at)] + [(self.r1.at[i], at) for i in range(3)]
+            sources = [(self.s0, own + at)] + [(self.r1.at[i], at) for i in range(2)]
             add_rows(self.s1, at, sources, self.piece, 16)
             if step:
                 src = self.s1.at[pl.ds(multiple(at, 16), self.piece), :]
@@ -187,9 +212,18 @@
     def back_first(self):
         p = self.p
         self.arrived()
-        at = p.core * self.half + p.first * self.quarter
-        mine = self.out.at[pl.ds(multiple(at, 16), self.quarter), :]
-        self.flight = [self.go(mine, mine, p.along_first(step)) for step in wire_steps]
+        mine = self.out.at[pl.ds(multiple(p.core * self.half, 16), self.half), :]
+        parts = [self.block(mine, p.first, part) for part in range(2)]
+        self.relayed = [self.go(parts[0], parts[0], p.along_first(1)), self.go(parts[1], parts[1], p.along_first(3))]
+        self.flight = [self.go(parts[1], parts[1], p.along_first(1)), self.go(parts[0], parts[0], p.along_first(3))]
+
+    def back_relay(self):
+        p = self.p
+        mine = self.out.at[pl.ds(multiple(p.core * self.half, 16), self.half), :]
+        for copy, step, part in ((self.relayed[0], 1, 0), (self.relayed[1], 3, 1)):
+            copy.wait_recv()
+            came = self.block(mine, lax.rem(p.first + ring_xy - step, ring_xy), part)
+            self.flight.append(self.go(came, came, p.along_first(step)))
 
     def back_pair(self):
         p = self.p
@@ -203,7 +237,7 @@
             copy.wait_send()
 
 
-copies_each = 28
+copies_each = 34
 stacks = ((0, 1024), (1024, 1024), (2048, 1024), (3072, 512))
 
 
@@ -304,9 +338,9 @@
 
 def step_kernel(
     scale,
-    field_in, taps_in, mix_in, up_in, down_in, cot_in,
+    field_in, taps_in, reach_in, mix_in, up_in, down_in, cot_in,
     block_rows, field_rows, total,
-    ext, gext, band, adjoint, tapx, revx, feats, cot, hidden, act_grad, act, pre_grad, mix, up, down,
+    ext, gext, band, adjoint, traw, far, tapx, revx, feats, cot, hidden, act_grad, act, pre_grad, mix, up, down,
     grads,
     load_sem, halo_send, halo_recv, grad_send, grad_recv, tap_send, tap_recv,
     *rest,
@@ -316,7 +350,8 @@
     own = slice(reach, reach + cols)
 
     loads = [
-        pltpu.make_async_copy(taps_in, tapx.at[:, 1 : rows + 1], load_sem.at[0]),
+        pltpu.make_async_copy(taps_in, traw, load_sem.at[0]),
+        pltpu.make_async_copy(reach_in, far, load_sem.at[6]),
         pltpu.make_async_copy(field_in, ext.at[1 : rows + 1, own], load_sem.at[1]),
         pltpu.make_async_copy(cot_in, cot, load_sem.at[2]),
         pltpu.make_async_copy(down_in, down, load_sem.at[3]),
@@ -332,7 +367,19 @@
 
     loads[0].wait()
 
+    loads[1].wait()
+    tap_at = lax.broadcasted_iota(jnp.int32, (taps, 2 * wide), 0)
+    spot_at = lax.broadcasted_iota(jnp.int32, (taps, 2 * wide), 1)
+    select = ((spot_at == tap_at) | (spot_at == wide + taps - 1 - tap_at)).astype(f32).astype(bf16)
+    away = jnp.abs(lax.broadcasted_iota(jnp.int32, (3, taps), 1) - reach)
+    revx[:, 1 : rows + 1] = jnp.zeros((basis, rows, 8, wide), f32)
+
     def build(r, carry):
+        for k in range(basis):
+            kept = jnp.where(away <= far[r], traw[k, r].astype(f32), 0.0).astype(bf16)
+            both = mm(kept, select)
+            tapx[k, r + 1, 0:3, :] = both[:, :wide]
+            revx[k, r + 1, 0:3, :] = both[:, wide:]
         for k in range(basis):
             for d in range(3):
                 band[r, k * cols : (k + 1) * cols, d * wide : (d + 1) * wide] = toeplitz(
@@ -341,19 +388,19 @@
         return carry
 
     lax.fori_loop(0, rows, build, 0)
-    loads[1].wait()
+    loads[2].wait()
     pl.semaphore_wait(barrier, len(devices))
     sent = halo.send(ext, halo_send, halo_recv)
     tap_copies = [
-        remote(tapx.at[:, 1], tapx.at[:, halo.side_n * (rows + 1)], tap_send.at[0], tap_recv.at[halo.side_n], halo.upper(0)),
-        remote(tapx.at[:, rows], tapx.at[:, halo.side_s * (rows + 1)], tap_send.at[1], tap_recv.at[halo.side_s], halo.lower(0)),
+        remote(revx.at[:, 1], revx.at[:, halo.side_n * (rows + 1)], tap_send.at[0], tap_recv.at[halo.side_n], halo.upper(0)),
+        remote(revx.at[:, rows], revx.at[:, halo.side_s * (rows + 1)], tap_send.at[1], tap_recv.at[halo.side_s], halo.lower(0)),
     ]
     for copy in tap_copies:
         copy.start()
     sent += tap_copies
 
-    loads[2].wait()
     loads[3].wait()
+    loads[4].wait()
 
     def early(i, carry):
         at = pl.ds(multiple(i * chunk, 16), chunk)
@@ -363,11 +410,6 @@
 
     lax.fori_loop(0, chunks, early, 0)
 
-    row_at = lax.broadcasted_iota(jnp.int32, (wide, wide), 0)
-    mirror = (row_at + lax.broadcasted_iota(jnp.int32, (wide, wide), 1) == taps - 1).astype(f32).astype(bf16)
-    straight = tapx[:, 1 : rows + 1].reshape(basis * rows * 8, wide).astype(bf16)
-    revx[:, 1 : rows + 1] = mm(straight, mirror).reshape(basis, rows, 8, wide)
-
     def build_back(r, carry):
         for k in range(basis):
             for s in range(3):
@@ -376,8 +418,8 @@
 
     lax.fori_loop(1, rows - 1, build_back, 0)
 
-    loads[4].wait()
     loads[5].wait()
+    loads[6].wait()
     halo.wait_columns(ext, halo_send, halo_recv)
 
     def features(r, carry):
@@ -457,17 +499,17 @@
     lax.fori_loop(0, 4, weight_mix, 0)
     sum_mix.start_pair()
     sum_up.pair_then_first()
+    sum_down.first_relay()
     lax.fori_loop(4, 6, weight_mix, 0)
     sum_rest.start_pair()
     sum_mix.pair_then_first()
+    sum_up.first_relay()
 
     for side in range(2):
-        here = tapx.at[:, side * (rows + 1)]
+        here = revx.at[:, side * (rows + 1)]
         remote(here, here, tap_send.at[0], tap_recv.at[side], halo.beside(1)).wait_recv()
     for r, pole in ((0, halo.top), (rows - 1, halo.bottom)):
         slot = 0 if r == 0 else rows + 1
-        straight = tapx[:, slot].reshape(basis * 8, wide).astype(bf16)
-        revx[:, slot] = mm(straight, mirror).reshape(basis, 8, wide)
         for k in range(basis):
             for s in range(3):
                 row = revx[k, r + s, 2 - s : 3 - s, :]
@@ -486,11 +528,12 @@
     halo.wait_columns(gext, grad_send, grad_recv)
     lax.fori_loop(1, rows // 2, pull, 0)
     sum_rest.pair_then_first()
+    sum_mix.first_relay()
     lax.fori_loop(rows // 2, rows - 1, pull, 0)
     halo.wait_rows(gext, grad_send, grad_recv)
     pull(0, 0)
     pull(rows - 1, 0)
-    sum_down.first_then_second()
+    sum_rest.first_relay()
 
     def last(i, carry):
         at = pl.ds(multiple(i * chunk, 16), chunk)
@@ -501,26 +544,19 @@
         return carry
 
     lax.fori_loop(0, 2, last, 0)
-    sum_up.first_then_second()
-    sum_down.second_then_z()
+    sum_down.first_then_second()
     lax.fori_loop(2, chunks, last, 0)
-    stages = ("first_then_second", "second_then_z", "z_then_back", "back_second", "back_first", "back_pair", "finish")
     order = (sum_down, sum_up, sum_mix, sum_rest)
-    done = {sum_down: 2, sum_up: 1, sum_mix: 0, sum_rest: 0}
-    for wave in range(2, len(stages) + len(order)):
-        for number in range(len(order)):
-            item, stage = order[number], wave - number
-            if done[item] <= stage < len(stages):
-                getattr(item, stages[stage])()
+    for item in order[1:]:
+        item.first_then_second()
+    for stage in ("second_then_z", "z_then_back", "back_second", "back_first", "back_relay", "back_pair", "finish"):
+        for item in order:
+            getattr(item, stage)()
     for copy in sent:
         copy.wait_send()
 
 
 def local(field_in, kernel_taps, row_reach, mix_weight, up_weight, down_weight, cotangent):
-    offsets = jnp.arange(wide, dtype=jnp.int32) - reach
-    mask = jnp.abs(offsets)[None, :] <= row_reach[:, None]
-    tap_rows = jnp.pad(kernel_taps, ((0, 0), (0, 0), (0, 5), (0, wide - taps))).astype(f32)
-    tap_rows = jnp.where(mask[None, :, None, :], tap_rows, 0.0)
     total_points = points * lax.axis_size("lat") * lax.axis_size("lon")
     scale = 1.0 / math.sqrt(total_points)
     anywhere = pl.BlockSpec(memory_space=pl.ANY)
@@ -533,13 +569,15 @@
         out_shape=(
             shape(field_in.shape, bf16), shape(field_in.shape, bf16), shape((3584, lanes), bf16),
         ),
-        in_specs=[anywhere] * 6,
+        in_specs=[anywhere] * 7,
         out_specs=(resident,) * 3,
         scratch_shapes=[
             v((rows + 2, wide, lanes), bf16),
             v((rows + 2, wide, lanes), bf16),
             v((rows, span, depth), bf16),
             v((rows, span, depth), bf16),
+            v((basis, rows, 3, taps), bf16),
+            pltpu.SMEM((rows,), jnp.int32),
             v((basis, rows + 2, 8, wide), f32),
             v((basis, rows + 2, 8, wide), f32),
             v((basis, points, lanes), bf16),
@@ -552,7 +590,7 @@
             v((lanes, hidden_units), bf16),
             v((hidden_units, lanes), bf16),
             v((3584, lanes), bf16),
-            dma((6,)), dma((8,)), dma((8,)), dma((8,)), dma((8,)), dma((2,)), dma((2,)),
+            dma((7,)), dma((8,)), dma((8,)), dma((8,)), dma((8,)), dma((2,)), dma((2,)),
         ]
         + [part for start, count in stacks for part in Reduction.scratch(count)]
         + [dma((copies_each,)) for _ in range(2 * len(stacks))],
@@ -560,7 +598,7 @@
             collective_id=0, has_side_effects=True, vmem_limit_bytes=vmem_room
         ),
         name="disco_step",
-    )(*[pltpu.with_memory_space_constraint(x, pltpu.HBM) for x in (field_in, tap_rows, mix_weight, up_weight, down_weight, cotangent)])
+    )(*[pltpu.with_memory_space_constraint(x, pltpu.HBM) for x in (field_in, kernel_taps, row_reach, mix_weight, up_weight, down_weight, cotangent)])
     return store_all(*[pltpu.with_memory_space_constraint(x, pltpu.VMEM) for x in made])
 
 

time: 92.5 us -> 83.3 us (0.901)
  Pallas kernels: 89.5 us -> 82.5 us
  other arithmetic: 2.16 us -> 0 us
    pallas_call x1, Pallas kernels: 87 us -> 80 us  [local(): pl.pallas_call(lambda *refs: step_kernel(scale, *refs), out_shape=(shape(...]
    select_n x1 -> x0, other arithmetic: 1.42 us -> none  [local(): tap_rows = jnp.where(mask[None, :, None, :], tap_rows, 0.0)]
where the time goes in v4:
time: 83.3 us; the launch traced here: 83.2 us
  Pallas kernels  82.5 us (99%)
    pallas_call x1, Pallas kernels, local(): pl.pallas_call(lambda *refs: step_kernel(scale, *refs), out_shape=(shape(...  80 us
    pallas_call x1, Pallas kernels, store_all(): pl.pallas_call(store_kernel, out_shape=(shape(block_rows.shape, bf16), sh...  2.53 us

profile of v4, /device:TPU:1, one launch (start us, length us, event | category | flops | bytes accessed | tf_op | source)
XLA Modules:
  0.0 83.2 jit_solution(16836980353184423809)
XLA Ops:
  0.6 80.0 %disco_step.1 = (bf16[10,96,512]{2,1,0:T(8,128)(2,1)S(1)}, bf16[10,96,512]{2,1,0:T(8,128)(2,1)S(1)}, bf16[3584,512]{1,0:T(8,128)(2,1)S(1)}) custom-call(bf16[10,96,512]{2,1,0:T(8,128)(2,1)} %refs_0_.1, bf16[3,10,3,33]{3,2,1,0:T(4,128)(2,1)} %refs_1_.1, s32[10]{0:T(128)} %refs_2_.1, bf16[3,512,512]{2,1,0:T(8,128)(2,1)} %refs_3_.1, bf16[512,1024]{1,0:T(8,128)(2,1)} %refs_4_.1, ...), custom_call_target="tpu_custom_call" | custom-call | tf_op jit(solution)/shard_map/disco_step/pallas_call | solution.py:567
  80.7 2.5 %store_all.1 = (bf16[10,96,512]{2,1,0:T(8,128)(2,1)}, bf16[10,96,512]{2,1,0:T(8,128)(2,1)}, bf16[3,512,512]{2,1,0:T(8,128)(2,1)}, bf16[512,1024]{1,0:T(8,128)(2,1)}, bf16[1024,512]{1,0:T(8,128)(2,1)}) custom-call(bf16[10,96,512]{2,1,0:T(8,128)(2,1)S(1)} %get-tuple-element.8.block_rows, bf16[10,96,512]{2,1,0:T(8,128)(2,1)S(1)} %get-tuple-element.9.field_rows, ...), custom_call_target="tpu_custom_call" | custom-call | tf_op jit(solution)/shard_map/store_all/pallas_call | solution.py:623

commit v5 on v4

--- a/solution.py
+++ b/solution.py
@@ -216,6 +216,8 @@
         parts = [self.block(mine, p.first, part) for part in range(2)]
         self.relayed = [self.go(parts[0], parts[0], p.along_first(1)), self.go(parts[1], parts[1], p.along_first(3))]
         self.flight = [self.go(parts[1], parts[1], p.along_first(1)), self.go(parts[0], parts[0], p.along_first(3))]
+        quarter = mine.at[pl.ds(multiple(p.first * self.quarter, 16), self.quarter), :]
+        self.handed = [self.go(quarter, quarter, p.partner())]
 
     def back_relay(self):
         p = self.p
@@ -224,12 +226,16 @@
             copy.wait_recv()
             came = self.block(mine, lax.rem(p.first + ring_xy - step, ring_xy), part)
             self.flight.append(self.go(came, came, p.along_first(step)))
+            self.handed.append(self.go(came, came, p.partner()))
 
     def back_pair(self):
         p = self.p
-        self.arrived()
         mine = self.out.at[pl.ds(multiple(p.core * self.half, 16), self.half), :]
-        self.flight = [self.go(mine, mine, p.partner())]
+        for copy, step, part in zip(self.flight, (3, 1, 2, 2), (1, 0, 0, 1)):
+            copy.wait_recv()
+            came = self.block(mine, lax.rem(p.first + step, ring_xy), part)
+            self.handed.append(self.go(came, came, p.partner()))
+        self.flight = self.handed
 
     def finish(self):
         self.arrived()
@@ -237,7 +243,7 @@
             copy.wait_send()
 
 
-copies_each = 34
+copies_each = 40
 stacks = ((0, 1024), (1024, 1024), (2048, 1024), (3072, 512))
 
 
@@ -250,7 +256,7 @@
 basis = 3
 points = rows * cols
 hidden_units = 1024
-chunk_rows = 2
+chunk_rows = 5
 chunk = chunk_rows * cols
 chunks = rows // chunk_rows
 span = basis * cols
@@ -525,15 +531,23 @@
             feats[k, at, :] = made[k * cols : (k + 1) * cols]
         return carry
 
-    halo.wait_columns(gext, grad_send, grad_recv)
-    lax.fori_loop(1, rows // 2, pull, 0)
     sum_rest.pair_then_first()
     sum_mix.first_relay()
-    lax.fori_loop(rows // 2, rows - 1, pull, 0)
+    sum_rest.first_relay()
+    sum_down.first_then_second()
+    sum_up.first_then_second()
+    halo.wait_columns(gext, grad_send, grad_recv)
+    lax.fori_loop(1, 4, pull, 0)
+    sum_mix.first_then_second()
+    sum_rest.first_then_second()
+    sum_down.second_then_z()
+    sum_up.second_then_z()
+    lax.fori_loop(4, rows - 1, pull, 0)
     halo.wait_rows(gext, grad_send, grad_recv)
     pull(0, 0)
     pull(rows - 1, 0)
-    sum_rest.first_relay()
+    sum_mix.second_then_z()
+    sum_rest.second_then_z()
 
     def last(i, carry):
         at = pl.ds(multiple(i * chunk, 16), chunk)
@@ -543,13 +557,12 @@
         field_rows[pl.ds(i * chunk_rows, chunk_rows)] = made.astype(bf16).reshape(chunk_rows, cols, lanes)
         return carry
 
-    lax.fori_loop(0, 2, last, 0)
-    sum_down.first_then_second()
-    lax.fori_loop(2, chunks, last, 0)
+    lax.fori_loop(0, 1, last, 0)
     order = (sum_down, sum_up, sum_mix, sum_rest)
-    for item in order[1:]:
-        item.first_then_second()
-    for stage in ("second_then_z", "z_then_back", "back_second", "back_first", "back_relay", "back_pair", "finish"):
+    for item in order:
+        item.z_then_back()
+    lax.fori_loop(1, chunks, last, 0)
+    for stage in ("back_second", "back_first", "back_relay", "back_pair", "finish"):
         for item in order:
             getattr(item, stage)()
     for copy in sent:

time: 83.3 us -> 79.5 us (0.954)
  Pallas kernels: 82.5 us -> 78.8 us
    pallas_call x1, Pallas kernels: 80 us -> 76.2 us  [local(): pl.pallas_call(lambda *refs: step_kernel(scale, *refs), out_shape=(shape(...]
where the time goes in v5:
time: 79.5 us; the launch traced here: 79.4 us
  Pallas kernels  78.8 us (99%)
    pallas_call x1, Pallas kernels, local(): pl.pallas_call(lambda *refs: step_kernel(scale, *refs), out_shape=(shape(...  76.2 us
    pallas_call x1, Pallas kernels, store_all(): pl.pallas_call(store_kernel, out_shape=(shape(block_rows.shape, bf16), sh...  2.53 us

profile of v5, /device:TPU:1, one launch (start us, length us, event | category | flops | bytes accessed | tf_op | source)
XLA Modules:
  0.0 79.4 jit_solution(2605557884486130834)
XLA Ops:
  0.6 76.2 %disco_step.1 = (bf16[10,96,512]{2,1,0:T(8,128)(2,1)S(1)}, bf16[10,96,512]{2,1,0:T(8,128)(2,1)S(1)}, bf16[3584,512]{1,0:T(8,128)(2,1)S(1)}) custom-call(bf16[10,96,512]{2,1,0:T(8,128)(2,1)} %refs_0_.1, bf16[3,10,3,33]{3,2,1,0:T(4,128)(2,1)} %refs_1_.1, s32[10]{0:T(128)} %refs_2_.1, bf16[3,512,512]{2,1,0:T(8,128)(2,1)} %refs_3_.1, bf16[512,1024]{1,0:T(8,128)(2,1)} %refs_4_.1, ...), custom_call_target="tpu_custom_call" | custom-call | tf_op jit(solution)/shard_map/disco_step/pallas_call | solution.py:580
  76.9 2.5 %store_all.1 = (bf16[10,96,512]{2,1,0:T(8,128)(2,1)}, bf16[10,96,512]{2,1,0:T(8,128)(2,1)}, bf16[3,512,512]{2,1,0:T(8,128)(2,1)}, bf16[512,1024]{1,0:T(8,128)(2,1)}, bf16[1024,512]{1,0:T(8,128)(2,1)}) custom-call(bf16[10,96,512]{2,1,0:T(8,128)(2,1)S(1)} %get-tuple-element.8.block_rows, bf16[10,96,512]{2,1,0:T(8,128)(2,1)S(1)} %get-tuple-element.9.field_rows, ...), custom_call_target="tpu_custom_call" | custom-call | tf_op jit(solution)/shard_map/store_all/pallas_call | solution.py:636

commit v6 on v5

--- a/solution.py
+++ b/solution.py
@@ -475,11 +475,11 @@
     sum_up, sum_down, sum_mix, sum_rest = sums
 
     def weight_down(i, carry):
-        part = pl.ds(multiple(i * 256, 256), 256)
-        grads[pl.ds(multiple(1024 + i * 256, 256), 256), :] = mm_tn(act[:, part], flat(cot)).astype(bf16)
-        return carry
-
-    lax.fori_loop(0, 4, weight_down, 0)
+        part = pl.ds(multiple(i * 512, 512), 512)
+        grads[pl.ds(multiple(1024 + i * 512, 512), 512), :] = mm_tn(act[:, part], flat(cot)).astype(bf16)
+        return carry
+
+    lax.fori_loop(0, 2, weight_down, 0)
     sum_down.start_pair()
 
     def weight_up(i, carry):
@@ -496,17 +496,15 @@
     sum_down.pair_then_first()
 
     def weight_mix(i, carry):
-        k, half = lax.div(i, 2), lax.rem(i, 2)
-        part = pl.ds(multiple(half * 256, 256), 256)
         grad = gext[1 : rows + 1, own].reshape(points, lanes)
-        grads[pl.ds(multiple(2048 + i * 256, 256), 256), :] = mm_tn(feats[k, :, part], grad).astype(bf16)
-        return carry
-
-    lax.fori_loop(0, 4, weight_mix, 0)
+        grads[pl.ds(multiple(2048 + i * 512, 512), 512), :] = mm_tn(feats[i], grad).astype(bf16)
+        return carry
+
+    lax.fori_loop(0, 2, weight_mix, 0)
     sum_mix.start_pair()
     sum_up.pair_then_first()
     sum_down.first_relay()
-    lax.fori_loop(4, 6, weight_mix, 0)
+    lax.fori_loop(2, 3, weight_mix, 0)
     sum_rest.start_pair()
     sum_mix.pair_then_first()
     sum_up.first_relay()

time: 79.5 us -> 79.3 us (level)
  no operation moved by 1% of the time
where the time goes in v6:
time: 79.3 us
  Pallas kernels  78.6 us (99%)
    pallas_call x1, Pallas kernels, local(): pl.pallas_call(lambda *refs: step_kernel(scale, *refs), out_shape=(shape(...  76.1 us
    pallas_call x1, Pallas kernels, store_all(): pl.pallas_call(store_kernel, out_shape=(shape(block_rows.shape, bf16), sh...  2.53 us

profile of v6, /device:TPU:1, one launch (start us, length us, event | category | flops | bytes accessed | tf_op | source)
XLA Modules:
  0.0 79.3 jit_solution(5673480793538357694)
XLA Ops:
  0.6 76.1 %disco_step.1 = (bf16[10,96,512]{2,1,0:T(8,128)(2,1)S(1)}, bf16[10,96,512]{2,1,0:T(8,128)(2,1)S(1)}, bf16[3584,512]{1,0:T(8,128)(2,1)S(1)}) custom-call(bf16[10,96,512]{2,1,0:T(8,128)(2,1)} %refs_0_.1, bf16[3,10,3,33]{3,2,1,0:T(4,128)(2,1)} %refs_1_.1, s32[10]{0:T(128)} %refs_2_.1, bf16[3,512,512]{2,1,0:T(8,128)(2,1)} %refs_3_.1, bf16[512,1024]{1,0:T(8,128)(2,1)} %refs_4_.1, ...), custom_call_target="tpu_custom_call" | custom-call | tf_op jit(solution)/shard_map/disco_step/pallas_call | solution.py:578
  76.7 2.5 %store_all.1 = (bf16[10,96,512]{2,1,0:T(8,128)(2,1)}, bf16[10,96,512]{2,1,0:T(8,128)(2,1)}, bf16[3,512,512]{2,1,0:T(8,128)(2,1)}, bf16[512,1024]{1,0:T(8,128)(2,1)}, bf16[1024,512]{1,0:T(8,128)(2,1)}) custom-call(bf16[10,96,512]{2,1,0:T(8,128)(2,1)S(1)} %get-tuple-element.8.block_rows, bf16[10,96,512]{2,1,0:T(8,128)(2,1)S(1)} %get-tuple-element.9.field_rows, ...), custom_call_target="tpu_custom_call" | custom-call | tf_op jit(solution)/shard_map/store_all/pallas_call | solution.py:634

commit v7 on v6

--- a/solution.py
+++ b/solution.py
@@ -393,10 +393,11 @@
                 )
         return carry
 
-    lax.fori_loop(0, rows, build, 0)
+    lax.fori_loop(0, 5, build, 0)
     loads[2].wait()
     pl.semaphore_wait(barrier, len(devices))
     sent = halo.send(ext, halo_send, halo_recv)
+    lax.fori_loop(5, rows, build, 0)
     tap_copies = [
         remote(revx.at[:, 1], revx.at[:, halo.side_n * (rows + 1)], tap_send.at[0], tap_recv.at[halo.side_n], halo.upper(0)),
         remote(revx.at[:, rows], revx.at[:, halo.side_s * (rows + 1)], tap_send.at[1], tap_recv.at[halo.side_s], halo.lower(0)),

time: 79.3 us -> 78.9 us (level)
  no operation moved by 1% of the time
where the time goes in v7:
time: 78.9 us; the launch traced here: 78.8 us
  Pallas kernels  78.1 us (99%)
    pallas_call x1, Pallas kernels, local(): pl.pallas_call(lambda *refs: step_kernel(scale, *refs), out_shape=(shape(...  75.6 us
    pallas_call x1, Pallas kernels, store_all(): pl.pallas_call(store_kernel, out_shape=(shape(block_rows.shape, bf16), sh...  2.53 us

profile of v7, /device:TPU:1, one launch (start us, length us, event | category | flops | bytes accessed | tf_op | source)
XLA Modules:
  0.0 78.8 jit_solution(10104386672199420318)
XLA Ops:
  0.6 75.6 %disco_step.1 = (bf16[10,96,512]{2,1,0:T(8,128)(2,1)S(1)}, bf16[10,96,512]{2,1,0:T(8,128)(2,1)S(1)}, bf16[3584,512]{1,0:T(8,128)(2,1)S(1)}) custom-call(bf16[10,96,512]{2,1,0:T(8,128)(2,1)} %refs_0_.1, bf16[3,10,3,33]{3,2,1,0:T(4,128)(2,1)} %refs_1_.1, s32[10]{0:T(128)} %refs_2_.1, bf16[3,512,512]{2,1,0:T(8,128)(2,1)} %refs_3_.1, bf16[512,1024]{1,0:T(8,128)(2,1)} %refs_4_.1, ...), custom_call_target="tpu_custom_call" | custom-call | tf_op jit(solution)/shard_map/disco_step/pallas_call | solution.py:579
  76.3 2.5 %store_all.1 = (bf16[10,96,512]{2,1,0:T(8,128)(2,1)}, bf16[10,96,512]{2,1,0:T(8,128)(2,1)}, bf16[3,512,512]{2,1,0:T(8,128)(2,1)}, bf16[512,1024]{1,0:T(8,128)(2,1)}, bf16[1024,512]{1,0:T(8,128)(2,1)}) custom-call(bf16[10,96,512]{2,1,0:T(8,128)(2,1)S(1)} %get-tuple-element.8.block_rows, bf16[10,96,512]{2,1,0:T(8,128)(2,1)S(1)} %get-tuple-element.9.field_rows, ...), custom_call_target="tpu_custom_call" | custom-call | tf_op jit(solution)/shard_map/store_all/pallas_call | solution.py:635
